TPU v7x, 32 devices: a whole 2x2x4 slice. The times are simulated.
32 devices in a mesh: dp: 16 (over z, y, x), tensor: 2 (over core).
Axes of the slice: x: 2, y: 2, z: 4, core: 2. Of those that a mesh axis runs over, the one named last changes fastest.
Arguments:
- incoming_embeddings: bfloat16 [16, 1024, 1024], P('dp', 'tensor'), may hold values from -6 to 6
- text_boundary_indicators: int32 [16, 1024], P('dp', 'tensor'), may hold values from 0 to 1, as said below
- upstream_sensitivity: bfloat16 [16, 1024, 1024], P('dp', 'tensor'), may hold values from -6 to 6
- primary_standardize_scaling: bfloat16 [1024], P(('dp', 'tensor')), may hold values from 0.5 to 1.5
- primary_standardize_offset: bfloat16 [1024], P(('dp', 'tensor')), may hold values from -1 to 1
- secondary_standardize_scaling: bfloat16 [1024], P(('dp', 'tensor')), may hold values from 0.5 to 1.5
- secondary_standardize_offset: bfloat16 [1024], P(('dp', 'tensor')), may hold values from -1 to 1
- feature_fading_logarithms: bfloat16 [1024], P(('dp', 'tensor')), may hold values from -8.6 to -3.2
- present_symbol_reward: bfloat16 [1024], P(('dp', 'tensor')), may hold values from -1 to 1
- timemix_lookup_blend: bfloat16 [1024], P(('dp', 'tensor')), may hold values from 0 to 1
- timemix_payload_blend: bfloat16 [1024], P(('dp', 'tensor')), may hold values from 0 to 1
- timemix_gate_blend: bfloat16 [1024], P(('dp', 'tensor')), may hold values from 0 to 1
- timemix_lookup_proj: bfloat16 [1024, 1024], P(('dp', 'tensor')), may hold values from -0.1875 to 0.1875
- timemix_payload_proj: bfloat16 [1024, 1024], P(('dp', 'tensor')), may hold values from -0.1875 to 0.1875
- timemix_gate_proj: bfloat16 [1024, 1024], P(('dp', 'tensor')), may hold values from -0.1875 to 0.1875
- timemix_emit_proj: bfloat16 [1024, 1024], P(('dp', 'tensor')), may hold values from -1.5 to 1.5
- feedmix_lookup_blend: bfloat16 [1024], P(('dp', 'tensor')), may hold values from 0 to 1
- feedmix_gate_blend: bfloat16 [1024], P(('dp', 'tensor')), may hold values from 0 to 1
- feedmix_gate_proj: bfloat16 [1024, 1024], P(('dp', 'tensor')), may hold values from -0.1875 to 0.1875
- feedmix_lookup_proj: bfloat16 [1024, 4096], P('dp', 'tensor'), may hold values from -0.1875 to 0.1875
- feedmix_payload_proj: bfloat16 [4096, 1024], P('tensor', 'dp'), may hold values from -0.09375 to 0.09375
Outputs:
- layer_out: bfloat16 [16, 1024, 1024], P('dp', 'tensor')
- grad_tokens: float32 [16, 1024, 1024], P('dp', 'tensor')
- grad_ln1_gain: float32 [1024], P(('dp', 'tensor'))
- grad_ln1_bias: float32 [1024], P(('dp', 'tensor'))
- grad_ln2_gain: float32 [1024], P(('dp', 'tensor'))
- grad_ln2_bias: float32 [1024], P(('dp', 'tensor'))
- grad_time_decay: float32 [1024], P(('dp', 'tensor'))
- grad_time_bonus: float32 [1024], P(('dp', 'tensor'))
- grad_att_mix_k: float32 [1024], P(('dp', 'tensor'))
- grad_att_mix_v: float32 [1024], P(('dp', 'tensor'))
- grad_att_mix_r: float32 [1024], P(('dp', 'tensor'))
- grad_att_key: float32 [1024, 1024], P(('dp', 'tensor'))
- grad_att_value: float32 [1024, 1024], P(('dp', 'tensor'))
- grad_att_recept: float32 [1024, 1024], P(('dp', 'tensor'))
- grad_att_out: float32 [1024, 1024], P(('dp', 'tensor'))
- grad_ffn_mix_k: float32 [1024], P(('dp', 'tensor'))
- grad_ffn_mix_r: float32 [1024], P(('dp', 'tensor'))
- grad_ffn_recept: float32 [1024, 1024], P(('dp', 'tensor'))
- grad_ffn_key: float32 [1024, 4096], P('dp', 'tensor')
- grad_ffn_value: float32 [4096, 1024], P('tensor', 'dp')
Inputs may be any that keep to these rules, and one draw needn't show every extreme that they name: `text_boundary_indicators`: position 0 of every row is a document start, and each row has at most 3 further starts.
All inputs are finite; a program needn't handle non-finite values.
Results may differ from a plain program's by a relative error of at most 0.02.
Values may be sent and summed in bfloat16 or wider, within the bound.
A program may use at most 192 MiB of HBM per device.

v0:
```python
import functools

import jax
import jax.numpy as jnp
from jax import lax
from jax.experimental import pallas as pl
from jax.experimental.pallas import tpu as pltpu
from jax.sharding import PartitionSpec as P

F32, BF16 = jnp.float32, jnp.bfloat16
MESH_ID = pl.DeviceIdType.MESH
MIB = 1 << 20
PARTS = 10
PIECES = 13


def place():
    i, c = lax.axis_index("dp"), lax.axis_index("tensor")
    return i // 4, i % 4, c


def neighbours(z, yx):
    x = yx + 1 - 2 * (yx % 2)
    y = (yx + 2) % 4
    d = (x + 2) % 4
    zs = (z + 1 - 2 * (z % 2), (z + 2) % 4, 3 - z)
    return x, y, d, zs


def enter(z, yx, c):
    x, y, d, zs = neighbours(z, yx)
    barrier = pltpu.get_barrier_semaphore()
    targets = [(z * 4 + yx, 1 - c), (z * 4 + x, c), (z * 4 + y, c)]
    targets += [(peer * 4 + yx, c) for peer in zs]
    for target in targets:
        pl.semaphore_signal(barrier, inc=1, device_id=target, device_id_type=MESH_ID)
    pl.semaphore_wait(barrier, len(targets))


def remote(src, dst, send, recv, target):
    return pltpu.make_async_remote_copy(
        src_ref=src, dst_ref=dst, send_sem=send, recv_sem=recv,
        device_id=target, device_id_type=MESH_ID,
    )


def strip(i, size):
    return pl.ds(pl.multiple_of(i * size, size), size)


class Gather:
    def __init__(self, view, sends, recvs, first=0):
        self.view, self.sends, self.recvs, self.first = view, sends, recvs, first
        self.z, self.yx, self.c = place()
        self.x, self.y, self.d, self.zs = neighbours(self.z, self.yx)

    def to(self, z, yx):
        return (z * 4 + yx, self.c)

    def copy(self, p, k, ref, target):
        return remote(ref, ref, self.sends.at[p, k], self.recvs.at[p, k], target)

    def along(self, p):
        own = self.view(p).at[self.z, self.yx]
        return [self.copy(p, k, own, self.to(peer, self.yx)) for k, peer in enumerate(self.zs)]

    def plane(self, p):
        own = self.view(p).at[:, self.yx]
        return [self.copy(p, 3, own, self.to(self.z, self.x)), self.copy(p, 4, own, self.to(self.z, self.y))]

    def onward(self, p):
        return [
            self.copy(p, 5, self.view(p).at[0:2, self.x], self.to(self.z, self.y)),
            self.copy(p, 6, self.view(p).at[2:4, self.y], self.to(self.z, self.x)),
        ]

    def start(self, copies):
        for copy in copies:
            copy.start()

    def arrive(self, copies):
        for copy in copies:
            copy.wait_recv()

    def step(self, p):
        self.arrive(self.along(p))
        self.start(self.plane(p))

    def forward(self, p):
        self.arrive(self.plane(p))
        self.start(self.onward(p))

    def finish(self, p):
        for copy in self.along(p) + self.plane(p) + self.onward(p):
            copy.wait_send()


class GatherLine(Gather):
    def ring(self, p):
        own = self.view(p).at[self.z, self.yx]
        return [self.copy(p, 0, own, self.to(self.z, self.x)), self.copy(p, 1, own, self.to(self.z, self.y))]

    def onward(self, p):
        half = self.view(p).shape[2] // 2
        return [
            self.copy(p, 2, self.view(p).at[self.z, self.x, 0:half], self.to(self.z, self.y)),
            self.copy(p, 3, self.view(p).at[self.z, self.y, half:], self.to(self.z, self.x)),
        ]

    def climb(self, p, k, up, arriving):
        behind = k if arriving else k - 1
        plane = self.z - behind if up else self.z + behind
        beyond = self.z + 1 if up != arriving else self.z - 1
        real = (plane >= 0) & (plane <= 3) & (beyond >= 0) & (beyond <= 3)
        plane, beyond = jnp.clip(plane, 0, 3), jnp.clip(beyond, 0, 3)
        k = (4 if up else 7) + k - 1
        return real, self.copy(p, k, self.view(p).at[plane], self.to(beyond, self.yx))

    def each(self, p, k, arriving, action):
        for up in (True, False):
            real, copy = self.climb(p, k, up, arriving)
            pl.when(real)(functools.partial(action, copy))

    def line(self, p, k):
        if k > 1:
            self.each(p, k - 1, True, lambda copy: copy.wait_recv())
        self.each(p, k, False, lambda copy: copy.start())

    def ready(self, p):
        self.each(p, 3, True, lambda copy: copy.wait_recv())

    def finish(self, p):
        for copy in self.ring(p) + self.onward(p):
            copy.wait_send()
        for k in (1, 2, 3):
            self.each(p, k, False, lambda copy: copy.wait_send())


class Reduce:
    def __init__(self, part, slot, ring1, ring2, line, out, sends, recvs):
        self.parts, self.slot, self.ring1, self.ring2, self.line, self.out = part, slot, ring1, ring2, line, out
        self.sends, self.recvs = sends, recvs
        self.z, self.yx, self.c = place()
        self.x, self.y, self.d, self.zs = neighbours(self.z, self.yx)

    def copy(self, k, src, dst, z, yx):
        return remote(src, dst, self.sends.at[k], self.recvs.at[k], (z * 4 + yx, self.c))

    def part(self):
        return self.parts.at[self.slot]

    def diagonal(self):
        return [
            self.copy(0, self.part().at[0:2, self.d], self.ring1.at[0], self.z, self.x),
            self.copy(1, self.part().at[2:4, self.d], self.ring1.at[1], self.z, self.y),
        ]

    def side(self):
        return [
            self.copy(2, self.part().at[:, self.x], self.ring2.at[0], self.z, self.x),
            self.copy(3, self.part().at[:, self.y], self.ring2.at[1], self.z, self.y),
        ]

    def down(self):
        return [
            self.copy(4 + k, self.part().at[peer, self.yx], self.line.at[k], peer, self.yx)
            for k, peer in enumerate(self.zs)
        ]

    def start(self, copies):
        for copy in copies:
            copy.start()

    def arrive(self, copies):
        for copy in copies:
            copy.wait_recv()

    def add_up(self, own, others, result):
        def step(i, carry):
            at = strip(i, 16)
            total = own[at, :].astype(F32)
            for other in others:
                total = total + other[at, :].astype(F32)
            result[at, :] = total.astype(result.dtype)
            return carry

        lax.fori_loop(0, own.shape[0] // 16, step, 0)

    def add(self, a, yx, others):
        own = self.part().at[a, yx]
        self.add_up(own, others, own)

    def stage1(self):
        self.start(self.diagonal())

    def stage2(self):
        self.arrive(self.diagonal())

        def planes(a, carry):
            self.add(a, self.y, [self.ring1.at[0, a]])
            self.add(a + 2, self.x, [self.ring1.at[1, a]])
            return carry

        lax.fori_loop(0, 2, planes, 0)
        self.start(self.side())

    def stage3(self):
        self.arrive(self.side())

        def planes(a, carry):
            self.add(a, self.yx, [self.ring2.at[0, a], self.ring2.at[1, a]])
            return carry

        lax.fori_loop(0, 4, planes, 0)
        self.start(self.down())

    def stage4(self):
        self.arrive(self.down())
        self.add_up(self.part().at[self.z, self.yx], [self.line.at[k] for k in range(3)], self.out)

    def finish(self):
        for copy in self.diagonal() + self.side() + self.down():
            copy.wait_send()


class ReduceLine(Reduce):
    def step(self, k, up, arriving):
        z = self.z
        plane = (3 if arriving else 4) - k + z if up else k - (3 if arriving else 4) + z
        beyond = z + 1 if up != arriving else z - 1
        real = (plane >= 0) & (plane <= 3) & (beyond >= 0) & (beyond <= 3)
        plane, beyond = jnp.clip(plane, 0, 3), jnp.clip(beyond, 0, 3)
        place_in = plane + 1 if up else plane
        k = (3 if up else 0) + k - 1
        return real, plane, place_in, self.copy(k, self.part().at[plane], self.line.at[place_in], beyond, self.yx)

    def take(self, arrived, plane, place_in):
        arrived.wait_recv()

        def blocks(yx, carry):
            self.add(plane, yx, [self.line.at[place_in, yx]])
            return carry

        lax.fori_loop(0, 4, blocks, 0)

    def move(self, k):
        for up in (True, False):
            real, plane, _, leaving = self.step(k, up, False)
            if k > 1:
                came, _, place_in, arrived = self.step(k - 1, up, True)

                pl.when(real & came)(functools.partial(self.take, arrived, plane, place_in))

            pl.when(real)(leaving.start)

    def halves(self):
        half = self.ring1.shape[1]
        own = self.part().at[self.z, self.d]
        return [
            self.copy(6, own.at[0:half], self.ring1.at[0], self.z, self.x),
            self.copy(7, own.at[half:], self.ring1.at[1], self.z, self.y),
        ]

    def sides(self):
        return [
            self.copy(8, self.part().at[self.z, self.x], self.ring2.at[0], self.z, self.x),
            self.copy(9, self.part().at[self.z, self.y], self.ring2.at[1], self.z, self.y),
        ]

    def stage1(self):
        self.move(1)

    def stage2(self):
        self.move(2)

    def stage3(self):
        self.move(3)

    def stage4(self):
        for up in (True, False):
            came, plane, place_in, arrived = self.step(3, up, True)
            pl.when(came)(functools.partial(self.take, arrived, plane, place_in))

        self.start(self.halves())

    def stage5(self):
        self.arrive(self.halves())
        half = self.ring1.shape[1]
        for yx, start, piece in ((self.y, 0, 0), (self.x, half, 1)):
            own = self.part().at[self.z, yx, start : start + half]
            self.add_up(own, [self.ring1.at[piece]], own)
        self.start(self.sides())

    def stage6(self):
        self.arrive(self.sides())
        self.add_up(self.part().at[self.z, self.yx], [self.ring2.at[0], self.ring2.at[1]], self.out)

    def finish(self):
        for k in (1, 2, 3):
            for up in (True, False):
                real, _, _, leaving = self.step(k, up, False)
                pl.when(real)(leaving.wait_send)
        for copy in self.halves() + self.sides():
            copy.wait_send()


def lanes(j):
    return slice(j * 128, (j + 1) * 128)


def bottom(v):
    return jnp.broadcast_to(v[7:8], v.shape)


def top(v):
    return jnp.broadcast_to(v[0:1], v.shape)


def masks_down(keep, place_in):
    m1 = jnp.where(place_in >= 1, keep, 0.0)
    m2 = m1 * pltpu.roll(m1, 1, 0)
    m4 = m2 * pltpu.roll(m2, 2, 0)
    for n in (1, 2, 4):
        keep = keep * jnp.where(place_in >= n, pltpu.roll(keep, n, 0), 1.0)
    return m1, m2, m4, keep


def masks_up(after, place_in):
    m1 = jnp.where(place_in <= 6, after, 0.0)
    m2 = m1 * pltpu.roll(m1, 7, 0)
    m4 = m2 * pltpu.roll(m2, 6, 0)
    for n in (1, 2, 4):
        after = after * jnp.where(place_in <= 7 - n, pltpu.roll(after, 8 - n, 0), 1.0)
    return m1, m2, m4, after


def wkv_forward(k_ref, v_ref, r_ref, keep_ref, rows_ref, mixed_ref, sn_ref, sd_ref):
    length, width = k_ref.shape
    tiles = width // 128
    place_in = lax.broadcasted_iota(jnp.int32, (8, 128), 0)
    first = place_in == 0
    zero = jnp.zeros((8, 128), F32)

    def pair(g, carry):
        carry = list(carry)
        base = pl.multiple_of(g * 16, 16)
        keeps = [keep_ref[pl.ds(base + 8 * h, 8), :] for h in range(2)]
        masks = [masks_down(keep, place_in) for keep in keeps]
        for j in range(tiles):
            d1, d2, d4, eu = (rows_ref[n : n + 1, lanes(j)] for n in range(4))
            dp = rows_ref[8:16, lanes(j)]
            made = []
            for h in range(2):
                at = pl.ds(base + 8 * h, 8)
                keep, (m1, m2, m4, mp) = keeps[h], masks[h]
                ek = jnp.exp(k_ref[at, lanes(j)])
                v = v_ref[at, lanes(j)]
                num, den = ek * v, ek
                x, b = num, eu * ek
                for n, coef in ((1, m1 * d1), (2, m2 * d2), (4, m4 * d4)):
                    num = num + coef * pltpu.roll(num, n, 0)
                    den = den + coef * pltpu.roll(den, n, 0)
                coef = mp * dp
                cn, cd = carry[2 * j], carry[2 * j + 1]
                num = num + coef * cn
                den = den + coef * cd
                sn = keep * jnp.where(first, cn, pltpu.roll(num, 1, 0))
                sd = keep * jnp.where(first, cd, pltpu.roll(den, 1, 0))
                carry[2 * j], carry[2 * j + 1] = bottom(num), bottom(den)
                sn_ref[at, lanes(j)] = sn
                sd_ref[at, lanes(j)] = sd
                weighted = (sn + eu * x) / (sd + b)
                made.append(jax.nn.sigmoid(r_ref[at, lanes(j)]) * weighted)
            mixed_ref[pl.ds(base, 16), lanes(j)] = jnp.concatenate(made, axis=0).astype(BF16)
        return tuple(carry)

    lax.fori_loop(0, length // 16, pair, (zero,) * (2 * tiles))


def wkv_backward(
    g_ref, k_ref, v_ref, r_ref, sn_ref, sd_ref, keep_ref, rows_ref, gk_ref, gv_ref, gr_ref, begin, end, carry
):
    length, width = k_ref.shape
    tiles = width // 128
    place_in = lax.broadcasted_iota(jnp.int32, (8, 128), 0)
    last = place_in == 7
    zero = jnp.zeros((8, 128), F32)
    pairs = length // 16

    def pair(step, carry):
        carry = list(carry)
        base = pl.multiple_of((pairs - 1 - step) * 16, 16)
        low, high = (keep_ref[pl.ds(base + 8 * h, 8), :] for h in range(2))
        afters = [
            jnp.where(last, top(high), pltpu.roll(low, 7, 0)),
            jnp.where(last, carry[4 * tiles], pltpu.roll(high, 7, 0)),
        ]
        masks = [masks_up(after, place_in) for after in afters]
        carry[4 * tiles] = top(low)
        for j in range(tiles):
            d1, d2, d4, eu = (rows_ref[n : n + 1, lanes(j)] for n in range(4))
            dp = rows_ref[16:24, lanes(j)]
            made = [None, None]
            for h in (1, 0):
                at = pl.ds(base + 8 * h, 8)
                after, (m1, m2, m4, mp) = afters[h], masks[h]
                ek = jnp.exp(k_ref[at, lanes(j)])
                v = v_ref[at, lanes(j)]
                sn, sd = sn_ref[at, lanes(j)], sd_ref[at, lanes(j)]
                s = jax.nn.sigmoid(r_ref[at, lanes(j)])
                b = eu * ek
                inverse = 1.0 / (sd + b)
                weighted = (sn + b * v) * inverse
                g = g_ref[at, lanes(j)]
                gs = g * s
                p = gs * inverse
                q = -p * weighted
                gr = gs * weighted * (1.0 - s)
                hp, hq = p, q
                for n, coef in ((1, m1 * d1), (2, m2 * d2), (4, m4 * d4)):
                    hp = hp + coef * pltpu.roll(hp, 8 - n, 0)
                    hq = hq + coef * pltpu.roll(hq, 8 - n, 0)
                coef = mp * dp
                cp, cq = carry[4 * j], carry[4 * j + 1]
                hp = hp + coef * cp
                hq = hq + coef * cq
                ap = after * jnp.where(last, cp, pltpu.roll(hp, 7, 0))
                aq = after * jnp.where(last, cq, pltpu.roll(hq, 7, 0))
                carry[4 * j], carry[4 * j + 1] = top(hp), top(hq)
                bonus = b * (v * p + q)
                gv = ek * ap + b * p
                gk = ek * (v * ap + aq) + bonus
                carry[4 * j + 2] = carry[4 * j + 2] + bonus
                carry[4 * j + 3] = carry[4 * j + 3] + (ap * sn + aq * sd)
                made[h] = (gk, gv, gr)
            both = pl.ds(base, 16)
            for n, ref in enumerate((gk_ref, gv_ref, gr_ref)):
                ref[both, lanes(j)] = jnp.concatenate([made[0][n], made[1][n]], axis=0).astype(BF16)
        return tuple(carry)

    return lax.fori_loop(begin, end, pair, (zero,) * (4 * tiles + 1) if carry is None else carry)


def wkv_sums(carry, rows_ref, decay_ref, bonus_ref):
    for j in range(decay_ref.shape[1] // 128):
        bonus_ref[0:1, lanes(j)] = jnp.sum(carry[4 * j + 2], axis=0, keepdims=True)
        decay_ref[0:1, lanes(j)] = -rows_ref[4:5, lanes(j)] * jnp.sum(carry[4 * j + 3], axis=0, keepdims=True)


NN, NT, TN = ((1,), (0,)), ((1,), (1,)), ((0,), (0,))
KEY, VALUE, GATE, EMIT, GATE2, FFN = 0, 1, 2, 3, 4, 5
KEYS, VALUES = (5, 7, 9, 11), (6, 8, 10, 12)
RINGS = 11
VECTORS = 11
TILE = 64
GAIN1, BIAS1, GAIN2, BIAS2, FADE, REWARD, MK1, MV1, MR1, MK2, MR2, OWN_FADE, OWN_REWARD = range(13)


def dot(a, b, dims):
    return lax.dot_general(a, b, (dims, ((), ())), preferred_element_type=F32)


def over_rows(length, size, body):
    def step(i, carry):
        body(strip(i, size))
        return carry

    lax.fori_loop(0, length // size, step, 0)


def matrix(ref):
    return ref[...].reshape(16 * ref.shape[2], ref.shape[3])


def emit_half(ref, h):
    rows = ref.shape[2] // 2
    return ref[:, :, h * rows : (h + 1) * rows, :].reshape(16 * rows, ref.shape[3])


def wide(column, width):
    return jnp.concatenate([column] * (width // 128), axis=1)


def norm(x):
    center = x - jnp.mean(x, axis=-1, keepdims=True)
    inverse = lax.rsqrt(jnp.mean(center * center, axis=-1, keepdims=True) + 1e-05)
    return center * inverse, inverse


def norm_and_mix(length, width, load, gain, bias, keep_ref, mixes, outs):
    first = lax.broadcasted_iota(jnp.int32, (TILE, width), 0) == 0

    def step(i, before):
        at = strip(i, TILE)
        unit, _ = norm(load(at))
        normed = unit * gain + bias
        prev = jnp.where(first, before, pltpu.roll(normed, 1, 0)) * wide(keep_ref[at, :], width)
        differ = normed - prev
        for share, out in zip(mixes, outs):
            out[at, :] = (prev + differ * share).astype(BF16)
        return normed[TILE - 1 : TILE]

    lax.fori_loop(0, length // TILE, step, jnp.zeros((1, width), F32))


def forward_kernel(
    own4, other4, rest, vec, x_own, up_own, keep_own,
    g_out, out, x_out, up_out, ins_out, kvr_out, sn_out, sd_out, mixed_out, resid_out, ins2_out, pre_out, act_out,
    gv_out, gr_out, vec_out, rows_out, keep_out,
    gv, g, x, up, ins, kvr, sn, sd, mixed, sum_own, sum_other, resid, ins2, pre, act, v_send, v_other, gval, grec, low_half,
    local_sem, ex_send, ex_recv, sends, recvs, lsends, lrecvs, vsends, vrecvs, out_sem, sum_send, sum_recv, val_send, val_recv,
):
    z, yx, c = place()
    length, width = x.shape
    half = width // 2
    span = length // 2
    partner = (z * 4 + yx, 1 - c)
    enter(z, yx, c)

    block = own4.shape[1]
    mine = strip(c, block)
    rows_mine = strip(c, span)
    swaps = [
        (vec, gv.at[z, yx, c]),
        (other4.at[0:3], g.at[0:3, z, yx, mine]),
        (other4.at[3], g.at[GATE2, z, yx, mine]),
        (x_own, x.at[rows_mine]),
        (keep_own, keep_out.at[rows_mine]),
        (up_own, up.at[rows_mine]),
    ]
    swaps = [remote(a, b, ex_send.at[n], ex_recv.at[n], partner) for n, (a, b) in enumerate(swaps)]
    keeps = [
        (vec, gv.at[z, yx, c]),
        (own4.at[0:3], g.at[0:3, z, yx, mine]),
        (own4.at[3], g.at[GATE2, z, yx, mine]),
        (x_own, x.at[rows_mine]),
        (keep_own, keep_out.at[rows_mine]),
        (up_own, up.at[rows_mine]),
        (rest.at[0], g.at[EMIT, z, yx]),
        (rest.at[1:9], g.at[FFN : FFN + 8, z, yx]),
    ]
    keeps = [pltpu.make_async_copy(a, b, local_sem.at[n]) for n, (a, b) in enumerate(keeps)]
    for copy in swaps + keeps:
        copy.start()
    weights = Gather(lambda p: g.at[p], sends, recvs)
    lines = GatherLine(lambda p: g.at[RINGS + p], lsends, lrecvs)
    vectors = Gather(lambda p: gv, vsends, vrecvs)

    outs = []

    def put(src, dst):
        copy = pltpu.make_async_copy(src, dst, out_sem.at[len(outs)])
        copy.start()
        outs.append(copy)
        return copy

    along_z = {4: [(0, 1)], 5: [(1, 1)], 6: [(0, 2)], 7: [(1, 2)], 8: [(0, 3)], 9: [(1, 3)]}

    def turn(n):
        if n < RINGS:
            weights.step(n)
            if n + 2 < RINGS:
                weights.start(weights.along(n + 2))
        if 1 <= n <= RINGS:
            weights.forward(n - 1)
        for p, k in along_z.get(n, []):
            lines.line(p, k)
        if n >= 2:
            weights.arrive(weights.onward(n - 2))
            put(g.at[n - 2], g_out.at[n - 2])

    def lined(p):
        lines.ready(p - RINGS)
        put(g.at[p], g_out.at[p])

    for copy in keeps[6:]:
        copy.wait()
    for p in range(PIECES - RINGS):
        lines.start(lines.ring(p))
    for n in (0, 1, 2):
        swaps[n].wait()
        keeps[n].wait()
    vectors.start(vectors.along(0))
    weights.start(weights.along(0))
    weights.start(weights.along(1))
    for p in range(PIECES - RINGS):
        lines.arrive(lines.ring(p))
        lines.start(lines.onward(p))
    vectors.step(0)
    turn(0)
    vectors.forward(0)
    for n in (3, 4, 5):
        swaps[n].wait()
        keeps[n].wait()
    x_copy, up_copy = put(x, x_out), put(up, up_out)
    for p in range(PIECES - RINGS):
        lines.arrive(lines.onward(p))
    turn(1)
    vectors.arrive(vectors.onward(0))

    for t in range(width // 128):
        parts = [gv[(2 * t + k) // 4, (2 * t + k) % 4, core].astype(F32) for k in range(2) for core in range(2)]
        vec_out[:, lanes(t)] = functools.reduce(lambda a, b: a + b, parts)
    ramp = lax.broadcasted_iota(jnp.int32, (8, 128), 0).astype(F32)
    for t in range(half // 128):
        own = functools.reduce(lambda a, b: a + b, [gv[t, k, c].astype(F32) for k in range(4)])
        rate = jnp.exp(own[OWN_FADE : OWN_FADE + 1])
        head = [
            jnp.exp(-rate), jnp.exp(-2.0 * rate), jnp.exp(-4.0 * rate), jnp.exp(own[OWN_REWARD : OWN_REWARD + 1]),
            rate * jnp.exp(-rate),
        ]
        for n, row in enumerate(head):
            rows_out[n : n + 1, lanes(t)] = row
        rows_out[8:16, lanes(t)] = jnp.exp(-(ramp + 1.0) * rate)
        rows_out[16:24, lanes(t)] = jnp.exp(-(8.0 - ramp) * rate)

    def row(n):
        return vec_out[n : n + 1, :]

    norm_and_mix(
        length, width, lambda at: x[at, :].astype(F32), row(GAIN1), row(BIAS1), keep_out,
        [row(MK1), row(MV1), row(MR1)], [ins.at[n] for n in range(3)],
    )
    put(ins, ins_out)
    kvr_copies = []
    for n in range(3):
        turn(n + 2)
        weight = g.at[n]

        def project(at):
            kvr[n, at, :] = dot(ins[n, at, :], matrix(weight), NN)

        over_rows(length, 256, project)
        kvr_copies.append(put(kvr.at[n], kvr_out.at[n]))
    wkv_forward(kvr.at[0], kvr.at[1], kvr.at[2], keep_out, rows_out, mixed, sn, sd)
    put(mixed, mixed_out)
    put(sn, sn_out)
    put(sd, sd_out)
    turn(5)
    weight = g.at[EMIT]
    quarters = length // 4

    def emitted(n):
        at = strip(n, quarters)
        return remote(sum_own.at[at], sum_other.at[at], sum_send.at[n], sum_recv.at[n], partner)

    def emit(n, carry):
        at = strip(n, quarters)
        for h in range(2):
            sum_own[at, h * half : (h + 1) * half] = dot(mixed[at, :], emit_half(weight, h), NN).astype(BF16)
        emitted(n).start()
        return carry

    lax.fori_loop(0, 4, emit, 0)
    turn(6)
    for n in range(4):
        emitted(n).wait()

    def add_up(at):
        total = x[at, :].astype(F32) + (sum_own[at, :].astype(F32) + sum_other[at, :].astype(F32))
        resid[0, at, :] = total[:, :half]
        resid[1, at, :] = total[:, half:]
        return total

    norm_and_mix(
        length, width, add_up, row(GAIN2), row(BIAS2), keep_out, [row(MK2), row(MR2)], [ins2.at[n] for n in range(2)]
    )
    put(resid, resid_out)
    put(ins2, ins2_out)
    for copy in kvr_copies:
        copy.wait()
    weight = g.at[GATE2]

    def gate(at):
        kvr[2, at, :] = jax.nn.sigmoid(dot(ins2[1, at, :], matrix(weight), NN))

    over_rows(length, 256, gate)
    pre_copies = []

    def expand_chunk(j):
        weight, slot = g.at[KEYS[j]], len(pre_copies) % 2
        if len(pre_copies) >= 2:
            pre_copies[-2].wait()

        def expand(at):
            positive = jnp.maximum(dot(ins2[0, at, :], matrix(weight), NN), 0.0)
            pre[slot, at, :] = positive.astype(BF16)
            act[j, at, :] = (positive * positive).astype(BF16)

        over_rows(length, 256, expand)
        pre_copies.append(put(pre.at[slot], pre_out.at[j]))
        put(act.at[j], act_out.at[j])

    def contract_chunk(j):
        weight = g.at[VALUES[j]]

        def contract(at):
            for h in range(2):
                part = dot(act[j, at, :], weight[2 * h : 2 * h + 2].reshape(half, -1), NT)
                kvr[h, at, :] = part if j == 0 else kvr[h, at, :] + part

        over_rows(length, 256, contract)

    turn(7)
    expand_chunk(0)
    turn(8)
    contract_chunk(0)
    turn(9)
    expand_chunk(1)
    turn(10)
    contract_chunk(1)
    lined(KEYS[3])
    expand_chunk(3)
    lined(VALUES[3])
    contract_chunk(3)
    turn(11)
    expand_chunk(2)
    turn(12)
    contract_chunk(2)

    columns = strip(c, half)

    def value_copy(n):
        at = strip(n, quarters)
        return remote(v_send.at[at], v_other.at[at], val_send.at[n], val_recv.at[n], partner)

    def back_copy(n):
        at = strip(n, quarters)
        return remote(gval.at[c, at], gval.at[c, at], val_send.at[4 + n], val_recv.at[4 + n], partner)

    def send_values(n, carry):
        def narrow(i, carry):
            at = strip(n * (quarters // 32) + i, 32)
            v_send[at, :] = kvr[1 - c, at, :].astype(BF16)
            return carry

        lax.fori_loop(0, quarters // 32, narrow, 0)
        value_copy(n).start()
        return carry

    def finish_values(n, carry):
        value_copy(n).wait()

        def finish(i, carry):
            at = strip(n * (quarters // 32) + i, 32)
            value = kvr[c, at, :] + v_other[at, :].astype(F32)
            s = kvr[2, at, :]
            low_half[at, :] = (resid[c, at, :] + s * value).astype(BF16)
            upstream = up[at, columns].astype(F32)
            gval[c, at, :] = (upstream * s).astype(BF16)
            grec[at, :] = (upstream * value * s * (1.0 - s)).astype(BF16)
            return carry

        lax.fori_loop(0, quarters // 32, finish, 0)
        back_copy(n).start()
        return carry

    lax.fori_loop(0, 4, send_values, 0)
    lax.fori_loop(0, 4, finish_values, 0)
    give = remote(low_half.at[strip(1 - c, span)], out.at[:, columns], val_send.at[8], val_recv.at[8], partner)
    give.start()
    put(low_half.at[rows_mine], out.at[:, columns])
    put(grec, gr_out)
    for n in range(4):
        back_copy(n).wait()
    put(gval, gv_out)
    give.wait()

    def close(p, carry):
        weights.finish(p)
        return carry

    lax.fori_loop(0, RINGS, close, 0)
    for p in range(PIECES - RINGS):
        lines.finish(p)
    vectors.finish(0)
    waited = kvr_copies + pre_copies[:2]
    for copy in outs:
        if not any(copy is other for other in waited):
            copy.wait()


def forward_call(own4, other4, rest, vec, x_own, up_own, keep_own):
    span, width = x_own.shape
    length, half = 2 * span, width // 2
    block = rest.shape[1:]
    any_, vmem = pl.BlockSpec(memory_space=pl.ANY), pl.BlockSpec(memory_space=pltpu.VMEM)
    full, col = (length, width), (length, half)

    def shape(dims, kind):
        return jax.ShapeDtypeStruct(dims, kind)

    outs = (
        (shape((PIECES, 4, 4) + block, BF16), any_),
        (shape((span, width), BF16), any_),
        (shape(full, BF16), any_),
        (shape(full, BF16), any_),
        (shape((3,) + full, BF16), any_),
        (shape((3,) + col, F32), any_),
        (shape(col, F32), any_),
        (shape(col, F32), any_),
        (shape(col, BF16), any_),
        (shape((2,) + col, F32), any_),
        (shape((2,) + full, BF16), any_),
        (shape((4,) + col, BF16), any_),
        (shape((4,) + col, BF16), any_),
        (shape((2,) + col, BF16), any_),
        (shape(col, BF16), any_),
        (shape((16, width), F32), vmem),
        (shape((24, half), F32), vmem),
        (shape((length, 128), F32), vmem),
    )
    dma = pltpu.SemaphoreType.DMA
    return pl.pallas_call(
        forward_kernel,
        out_shape=tuple(o[0] for o in outs),
        in_specs=[vmem] * 7,
        out_specs=tuple(o[1] for o in outs),
        scratch_shapes=[
            pltpu.VMEM((4, 4, 2) + vec.shape, BF16),
            pltpu.VMEM((PIECES, 4, 4) + block, BF16),
            pltpu.VMEM(full, BF16),
            pltpu.VMEM(full, BF16),
            pltpu.VMEM((3,) + full, BF16),
            pltpu.VMEM((3,) + col, F32),
            pltpu.VMEM(col, F32),
            pltpu.VMEM(col, F32),
            pltpu.VMEM(col, BF16),
            pltpu.VMEM(full, BF16),
            pltpu.VMEM(full, BF16),
            pltpu.VMEM((2,) + col, F32),
            pltpu.VMEM((2,) + full, BF16),
            pltpu.VMEM((2,) + col, BF16),
            pltpu.VMEM((4,) + col, BF16),
            pltpu.VMEM(col, BF16),
            pltpu.VMEM(col, BF16),
            pltpu.VMEM((2,) + col, BF16),
            pltpu.VMEM(col, BF16),
            pltpu.VMEM(col, BF16),
            dma((8,)), dma((6,)), dma((6,)),
            dma((RINGS, 7)), dma((RINGS, 7)), dma((PIECES - RINGS, 10)), dma((PIECES - RINGS, 10)), dma((1, 7)), dma((1, 7)),
            dma((40,)), dma((4,)), dma((4,)), dma((9,)), dma((9,)),
        ],
        compiler_params=pltpu.CompilerParams(
            collective_id=0, has_side_effects=True, vmem_limit_bytes=63 * MIB
        ),
        name="forward",
    )(own4, other4, rest, vec, x_own, up_own, keep_own)


R_VALUE, R_KEY, R_GATE2, R_EMIT, R_TIME = 0, 4, 8, 9, 10
WEIGHT_ORDER = [p for j in range(4) for p in (VALUES[j], KEYS[j])] + [GATE2, EMIT, KEY, VALUE, GATE]
LINED = (1, 3, 5)
SUMS = 11
S_GAIN1, S_BIAS1, S_GAIN2, S_BIAS2, S_DECAY, S_BONUS, S_MK1, S_MV1, S_MR1, S_MK2, S_MR2 = range(11)
SLOTS = 12


def whole(ref, at):
    return jnp.concatenate([ref[0, at, :], ref[1, at, :]], axis=1)


def halves(ref, at, value):
    half = value.shape[1] // 2
    ref[0, at, :] = value[:, :half].astype(ref.dtype)
    ref[1, at, :] = value[:, half:].astype(ref.dtype)


def fold(value):
    return sum(value[n : n + 8] for n in range(8, value.shape[0], 8)) + value[:8]


def back_through_norm(g, unit, inverse, gain):
    q = g * gain
    return inverse * (
        q - jnp.mean(q, axis=-1, keepdims=True) - unit * jnp.mean(q * unit, axis=-1, keepdims=True)
    )


def lifted(now, following, last):
    return jnp.where(last, following[0:1], pltpu.roll(now, now.shape[0] - 1, 0))


def backward_kernel(
    plan,
    g, x_in, up_in, ins_in, kvr_in, sn_in, sd_in, mixed_in, resid_in, ins2_in, pre_in, act_in, gv_in, gr_in,
    vec, rows, keep,
    out, recv4, vsum, vother, gtok,
    part, ring1, ring2, line, lring1, lring2, lline, vpart, vring1, vring2, vline,
    b, w, f, resid, sum_other, n1_other, acc, own_sums,
    load_sem, w_sem, sends, recvs, lsends, lrecvs, vsends, vrecvs, ex_send, ex_recv, sum_send, sum_recv,
):
    z, yx, c = place()
    nx, ny, nd, zs = neighbours(z, yx)
    length, half = b.shape[1:]
    width = 2 * half
    span = length // 2
    quarter = length // 4
    partner = (z * 4 + yx, 1 - c)
    loads = {}

    def load(name, src, dst):
        copy = pltpu.make_async_copy(src, dst, load_sem.at[len(loads)])
        copy.start()
        loads[name] = copy

    def loaded(*names):
        for name in names:
            loads[name].wait()

    def pair(n):
        return b.at[n : n + 2]

    def load_pair(name, src, n):
        for h in range(2):
            load((name, h), src.at[:, h * half : (h + 1) * half], b.at[n + h])

    def loaded_pair(name):
        loaded((name, 0), (name, 1))

    def weight_copy(n):
        return pltpu.make_async_copy(g.at[WEIGHT_ORDER[n]], w.at[n % 3], w_sem.at[n])

    def weight(n):
        weight_copy(n).wait()
        return w.at[n % 3]

    GVAL, ACT, PRE, IN_K2, IN_R2, GREC, GPRE = 0, 2, 4, 6, 8, 10, 11
    load("gv0", gv_in.at[0], b.at[GVAL])
    load("gv1", gv_in.at[1], b.at[GVAL + 1])
    for j in range(2):
        load(("act", j), act_in.at[j], b.at[ACT + j])
    load_pair("in_k2", ins2_in.at[0], IN_K2)
    for j in range(2):
        load(("pre", j), pre_in.at[j], b.at[PRE + j])
    for n in range(3):
        weight_copy(n).start()
    load_pair("in_r2", ins2_in.at[1], IN_R2)
    load("gr", gr_in, b.at[GREC])
    load("resid", resid_in, resid)
    enter(z, yx, c)

    sums = []
    for p in range(PIECES):
        if p in LINED:
            n = LINED.index(p)
            sums.append(
                ReduceLine(
                    part, p % PARTS, lring1.at[n], lring2.at[n], lline.at[n], out.at[p], lsends.at[n], lrecvs.at[n]
                )
            )
        else:
            n = p - sum(q < p for q in LINED)
            sums.append(
                Reduce(part, p % PARTS, ring1.at[n], ring2.at[n], line.at[n], out.at[p], sends.at[n], recvs.at[n])
            )
    vector_sums = Reduce(vpart, 0, vring1, vring2, vline, vsum, vsends, vrecvs)
    final = []
    rows4 = recv4.shape[1]
    others = strip(1 - c, rows4)

    def pump(name):
        for stage, p in plan[name]:
            if p == "v":
                getattr(vector_sums, "stage%d" % stage)()
                continue
            getattr(sums[p], "stage%d" % stage)()
            if stage == 4 and p in (R_GATE2, R_TIME, R_TIME + 1, R_TIME + 2):
                n = len(final)
                slot = 3 if p == R_GATE2 else p - R_TIME
                final.append(remote(out.at[p, others], recv4.at[slot], ex_send.at[n], ex_recv.at[n], partner))
                final[-1].start()

    def gradient(p, lhs, rhs):
        def block(a, carry):
            rows_a = dot(lhs[a // 2, :, strip(a % 2, half // 2)], rhs[...], TN)
            part[p % PARTS, a] = rows_a.astype(BF16).reshape(part.shape[2:])
            return carry

        lax.fori_loop(0, 4, block, 0)

    def thirds(ref, h):
        return ref[2 * h : 2 * h + 2].reshape(half, half)

    loaded("gv0", "gv1")
    for j in range(4):
        loaded(("act", j))
        gradient(R_VALUE + j, pair(GVAL), b.at[ACT + j % 2])
        if j < 2:
            load(("act", j + 2), act_in.at[j + 2], b.at[ACT + j])
        pump("fv%d" % j)
    loaded_pair("in_k2")
    for j in range(4):
        loaded(("pre", j))
        value_w = weight(2 * j)

        def through(at):
            g_hidden = sum(dot(b[GVAL + h, at, :], thirds(value_w, h), NN) for h in range(2))
            b[GPRE, at, :] = (2.0 * b[PRE + j % 2, at, :].astype(F32) * g_hidden).astype(BF16)

        over_rows(length, 256, through)
        pump("th%d" % j)
        if j < 2:
            load(("pre", j + 2), pre_in.at[j + 2], b.at[PRE + j])
        weight_copy(2 * j + 3).start()
        gradient(R_KEY + j, pair(IN_K2), b.at[GPRE])
        pump("fk%d" % j)
        key_w = weight(2 * j + 1)

        def collect(at):
            for h in range(2):
                piece = dot(b[GPRE, at, :], thirds(key_w, h), NT)
                f[h, at, :] = piece if j == 0 else f[h, at, :] + piece

        over_rows(length, 256, collect)
        pump("co%d" % j)
        weight_copy(2 * j + 4).start()
    loaded_pair("in_r2")
    loaded("gr")
    gradient(R_GATE2, pair(IN_R2), b.at[GREC])
    pump("g2")
    gate_w = weight(8)

    def gate_back(at):
        for h in range(2):
            f[2 + h, at, :] = dot(b[GREC, at, :], thirds(gate_w, h), NT)

    over_rows(length, 256, gate_back)
    pump("gb")
    weight_copy(11).start()
    loaded("resid")

    SUM_OWN, UP, BRANCH, MIXED, G3, X, IN_K, IN_V, IN_R, SEND = 0, 2, 4, 6, 7, 4, 10, 0, 2, 6
    load_pair("up", up_in, UP)
    load("mixed", mixed_in, b.at[MIXED])
    acc[...] = jnp.zeros_like(acc)
    last = lax.broadcasted_iota(jnp.int32, (TILE, width), 0) == TILE - 1

    def row(n):
        return vec[n : n + 1, :]

    def kept(at, n):
        return wide(keep[at, :], width) if n is None else wide(keep[n, :], width)

    gain2, bias2, mk2, mr2 = (GAIN2, BIAS2, MK2, MR2)
    sum_copies = []
    for q in range(4):

        def tile(i, carry):
            base = q * quarter + i * TILE
            at = pl.ds(pl.multiple_of(base, TILE), TILE)
            after = pl.ds(pl.multiple_of(jnp.minimum(base + TILE, length - 8), 8), 8)
            inside = jnp.where(base + TILE < length, 1.0, 0.0)
            keep_at, keep_after = wide(keep[at, :], width), wide(keep[after, :], width) * inside
            unit, _ = norm(whole(resid, at))
            normed = unit * row(gain2) + row(bias2)
            total = jnp.zeros_like(unit)
            for n, share in enumerate((mk2, mr2)):
                back = whole(f.at[2 * n : 2 * n + 2], at)
                ahead = lifted(back * keep_at, whole(f.at[2 * n : 2 * n + 2], after) * keep_after, last)
                total = total + ahead + (back - ahead) * row(share)
                acc[S_MK2 + n] = acc[S_MK2 + n] + fold(normed * (back - ahead))
            acc[S_GAIN2] = acc[S_GAIN2] + fold(total * unit)
            acc[S_BIAS2] = acc[S_BIAS2] + fold(total)
            halves(b.at[SUM_OWN : SUM_OWN + 2], at, total)
            return carry

        lax.fori_loop(0, quarter // TILE, tile, 0)
        at = pl.ds(q * quarter, quarter)
        sum_copies.append(
            remote(b.at[SUM_OWN : SUM_OWN + 2, at], sum_other.at[:, at], sum_send.at[q], sum_recv.at[q], partner)
        )
        sum_copies[-1].start()
        pump("a%d" % q)
    for n in range(3):
        load(("kvr", n), kvr_in.at[n], f.at[n])
    load("sn", sn_in, f.at[3])
    load("sd", sd_in, f.at[4])
    load_pair("in_k", ins_in.at[0], IN_K)

    loaded_pair("up")
    for q in range(4):
        sum_copies[q].wait_recv()

        def tile(i, carry):
            at = pl.ds(pl.multiple_of(q * quarter + i * TILE, TILE), TILE)
            unit, inverse = norm(whole(resid, at))
            total = whole(b.at[SUM_OWN : SUM_OWN + 2], at).astype(F32) + whole(sum_other, at).astype(F32)
            back = whole(pair(UP), at).astype(F32) + back_through_norm(total, unit, inverse, row(gain2))
            halves(pair(BRANCH), at, back)

            @pl.when(c == q // 2)
            def _():
                gtok[pl.ds(pl.multiple_of((q % 2) * quarter + i * TILE, TILE), TILE), :] = back

            return carry

        lax.fori_loop(0, quarter // TILE, tile, 0)
        pump("b%d" % q)
    for copy in sum_copies:
        copy.wait_send()
    load_pair("in_v", ins_in.at[1], IN_V)
    load_pair("in_r", ins_in.at[2], IN_R)

    loaded("mixed")
    rows_h = part.shape[3] // 2
    for h in range(2):

        def emit_rows(a, carry):
            block = dot(b[MIXED, :, strip(a, half // 2)], b[BRANCH + h], TN).astype(BF16)
            part[R_EMIT, pl.ds(2 * a, 2), :, h * rows_h : (h + 1) * rows_h, :] = block.reshape(2, 4, rows_h, half)
            return carry

        lax.fori_loop(0, 2, emit_rows, 0)
    pump("em")
    emit_w = weight(9)

    def emit_back(at):
        resid[0, at, :] = sum(dot(b[BRANCH + h, at, :], emit_half(emit_w, h), NT) for h in range(2))

    over_rows(length, 256, emit_back)
    pump("eb")
    weight_copy(12).start()
    load_pair("x", x_in, X)

    loaded(("kvr", 0), ("kvr", 1), ("kvr", 2), "sn", "sd")
    carry = None
    for q in range(4):
        carry = wkv_backward(
            resid.at[0], f.at[0], f.at[1], f.at[2], f.at[3], f.at[4], keep, rows, b.at[G3], b.at[G3 + 1], b.at[G3 + 2],
            q * (length // 64), (q + 1) * (length // 64), carry,
        )
        pump("w%d" % q)
    wkv_sums(carry, rows, own_sums.at[0:1], own_sums.at[1:2])

    for n, (name, slot) in enumerate((("in_k", IN_K), ("in_v", IN_V), ("in_r", IN_R))):
        loaded_pair(name)
        sums[R_TIME + n - PARTS].finish()
        gradient(R_TIME + n, pair(slot), b.at[G3 + n])
        pump("t%d" % n)
    loaded_pair("x")
    for n in range(3):
        weight(10 + n)
    for n in range(3):
        for h in range(2):
            f[n, pl.ds(h * span + quarter, 8), :] = jnp.zeros((8, half), F32)
    n1_copies = []
    for q in (3, 2, 1, 0):
        def back_rows(n, carry):
            for h in range(2):
                if q < 3:
                    f[n, pl.ds(h * span + quarter, 8), :] = f[n, pl.ds(h * span, 8), :]
                f[n, pl.ds(h * span, quarter), :] = dot(
                    b[G3 + n, pl.ds(q * quarter, quarter), :], thirds(w.at[(n + 1) % 3], h), NT
                )
            return carry

        lax.fori_loop(0, 3, back_rows, 0)

        def tile(i, carry):
            base = q * quarter + i * TILE
            at = pl.ds(pl.multiple_of(base, TILE), TILE)
            after = pl.ds(pl.multiple_of(jnp.minimum(base + TILE, length - 8), 8), 8)
            keep_at, keep_after = wide(keep[at, :], width), wide(keep[after, :], width)

            def take(n, start, size):
                return jnp.concatenate(
                    [f[n, pl.ds(pl.multiple_of(h * span + start, 8), size), :] for h in range(2)], axis=1
                )

            unit, _ = norm(whole(pair(X), at).astype(F32))
            normed = unit * row(GAIN1) + row(BIAS1)
            total = jnp.zeros_like(unit)
            for n, share in enumerate((MK1, MV1, MR1)):
                back = take(n, i * TILE, TILE)
                ahead = lifted(back * keep_at, take(n, i * TILE + TILE, 8) * keep_after, last)
                total = total + ahead + (back - ahead) * row(share)
                acc[S_MK1 + n] = acc[S_MK1 + n] + fold(normed * (back - ahead))
            acc[S_GAIN1] = acc[S_GAIN1] + fold(total * unit)
            acc[S_BIAS1] = acc[S_BIAS1] + fold(total)
            rows_q = [pl.ds(pl.multiple_of(h * span + (q % 2) * quarter + i * TILE, TILE), TILE) for h in range(2)]

            @pl.when(c == q // 2)
            def _():
                for h in range(2):
                    f[3, rows_q[h], :] = total[:, h * half : (h + 1) * half]

            @pl.when(c != q // 2)
            def _():
                for h in range(2):
                    b[SEND, rows_q[h], :] = total[:, h * half : (h + 1) * half].astype(BF16)

            return carry

        lax.fori_loop(0, quarter // TILE, tile, 0)
        pump("c%d" % (3 - q))
    swap_n1 = remote(b.at[SEND], n1_other, sum_send.at[4], sum_recv.at[4], partner)
    swap_n1.start()

    for n in (S_GAIN1, S_BIAS1, S_GAIN2, S_BIAS2, S_MK1, S_MV1, S_MR1, S_MK2, S_MR2):
        acc[n, 0:1, :] = jnp.sum(acc[n], axis=0, keepdims=True)
    for i in range(16):
        vpart[0, i // 4, i % 4] = jnp.concatenate(
            [acc[n, 0:1, lanes(i // 2)] for n in range(SUMS)]
            + [own_sums[n : n + 1, lanes(i // 4)] for n in range(2)]
            + [jnp.zeros((3, 128), F32)]
        )
    pump("v0")
    swap_n1.wait()

    def tokens(i, carry):
        at = strip(i, TILE)
        spans = [pl.ds(pl.multiple_of(h * span + i * TILE, TILE), TILE) for h in range(2)]
        unit, inverse = norm(whole(pair(X), pl.ds(pl.multiple_of(c * span + i * TILE, TILE), TILE)).astype(F32))
        total = jnp.concatenate([f[3, s, :] + n1_other[s, :].astype(F32) for s in spans], axis=1)
        gtok[at, :] = gtok[at, :] + back_through_norm(total, unit, inverse, row(GAIN1))
        return carry

    lax.fori_loop(0, span // TILE, tokens, 0)
    for n in range(1, 4):
        pump("v%d" % n)
    swap = remote(vsum, vother, ex_send.at[4], ex_recv.at[4], partner)
    swap.start()
    pump("end")
    for p in range(PIECES - PARTS, PIECES):
        sums[p].finish()
    vector_sums.finish()
    for copy in final + [swap]:
        copy.wait()


PLAN = {
    "fv0": [(1, 0)],
    "fv1": [(1, 1)],
    "fv2": [(1, 2)],
    "fv3": [(1, 3), (2, 0)],
    "th0": [],
    "fk0": [(1, 4), (2, 2), (2, 1)],
    "co0": [],
    "th1": [],
    "fk1": [(1, 5), (3, 0), (2, 3)],
    "co1": [(2, 4)],
    "th2": [(3, 1)],
    "fk2": [(1, 6), (3, 2)],
    "co2": [],
    "th3": [(2, 5)],
    "fk3": [(1, 7), (3, 4)],
    "co3": [(2, 6), (4, 0)],
    "g2": [(1, 8), (2, 7)],
    "gb": [],
    "a0": [(3, 3)],
    "a1": [],
    "a2": [(3, 6)],
    "a3": [(4, 1), (2, 8)],
    "b0": [(3, 7), (5, 1), (4, 2)],
    "b1": [],
    "b2": [],
    "b3": [(3, 5), (3, 8)],
    "em": [(1, 9), (6, 1)],
    "eb": [],
    "w0": [(4, 4)],
    "w1": [(2, 9)],
    "w2": [(4, 3)],
    "w3": [],
    "t0": [(1, 10)],
    "t1": [(1, 11), (5, 3), (3, 9), (4, 6)],
    "t2": [(1, 12)],
    "c0": [(2, 10), (2, 11), (6, 3), (4, 7)],
    "c1": [(4, 5), (2, 12)],
    "c2": [(3, 10), (4, 8)],
    "c3": [],
    "v0": [(1, "v"), (3, 11), (5, 5)],
    "v1": [(2, "v"), (4, 9), (4, 10), (3, 12)],
    "v2": [(3, "v"), (6, 5), (4, 11)],
    "v3": [(4, "v")],
    "end": [(4, 12)],
}


def backward_call(g, x, up, ins, kvr, sn, sd, mixed, resid, ins2, pre, act, g_value, g_recept, vec, rows, keep):
    block = g.shape[3:]
    length, half = sn.shape
    lined = len(LINED)
    rings = PIECES - lined
    any_, vmem = pl.BlockSpec(memory_space=pl.ANY), pl.BlockSpec(memory_space=pltpu.VMEM)
    dma = pltpu.SemaphoreType.DMA

    def shape(*dims):
        return jax.ShapeDtypeStruct(dims, F32)

    return pl.pallas_call(
        functools.partial(backward_kernel, PLAN),
        out_shape=(
            shape(PIECES, *block), shape(4, block[0] // 2, block[1]), shape(16, 128), shape(16, 128),
            shape(length // 2, 2 * half),
        ),
        in_specs=[any_] * 14 + [vmem] * 3,
        out_specs=(vmem,) * 5,
        scratch_shapes=[
            pltpu.VMEM((PARTS, 4, 4) + block, BF16),
            pltpu.VMEM((rings, 2, 2) + block, BF16),
            pltpu.VMEM((rings, 2, 4) + block, BF16),
            pltpu.VMEM((rings, 3) + block, BF16),
            pltpu.VMEM((lined, 2, block[0] // 2, block[1]), BF16),
            pltpu.VMEM((lined, 2) + block, BF16),
            pltpu.VMEM((lined, 5, 4) + block, BF16),
            pltpu.VMEM((1, 4, 4, 16, 128), F32),
            pltpu.VMEM((2, 2, 16, 128), F32),
            pltpu.VMEM((2, 4, 16, 128), F32),
            pltpu.VMEM((3, 16, 128), F32),
            pltpu.VMEM((SLOTS, length, half), BF16),
            pltpu.VMEM((3, 4, 4) + block, BF16),
            pltpu.VMEM((5, length, half), F32),
            pltpu.VMEM((2, length, half), F32),
            pltpu.VMEM((2, length, half), BF16),
            pltpu.VMEM((length, half), BF16),
            pltpu.VMEM((SUMS, 8, 2 * half), F32),
            pltpu.VMEM((8, half), F32),
            dma((40,)), dma((PIECES,)), dma((rings, 7)), dma((rings, 7)), dma((lined, 10)), dma((lined, 10)),
            dma((7,)), dma((7,)), dma((5,)), dma((5,)), dma((5,)), dma((5,)),
        ],
        compiler_params=pltpu.CompilerParams(collective_id=1, has_side_effects=True, vmem_limit_bytes=63 * MIB),
        name="backward",
    )(g, x, up, ins, kvr, sn, sd, mixed, resid, ins2, pre, act, g_value, g_recept, vec, rows, keep)


def shifted(value, axis, steps):
    count = lax.axis_size(axis)
    first, last = (max(0, -steps), min(count, count - steps))
    return lax.ppermute(value, axis, [(source, source + steps) for source in range(first, last)])


def carried_in(array, axis, join, neutral):
    place = lax.axis_index(axis)
    gathered = jax.tree.map(
        lambda a, kind: lax.all_gather(a.astype(kind), axis),
        array,
        (jnp.bfloat16, jnp.bfloat16, jnp.bfloat16),
    )
    state = jax.tree.map(lambda a, e: jnp.zeros_like(a) + jnp.asarray(e, a.dtype), array, neutral)

    def one(turn, state):
        return join(
            state,
            jax.tree.map(
                lambda a, own: lax.dynamic_index_in_dim(a, turn, 0, False).astype(own.dtype),
                gathered,
                array,
            ),
        )

    return lax.fori_loop(0, place, one, state)


def entering(array, axis, combine, identity):
    count, place = (lax.axis_size(axis), lax.axis_index(axis))
    everything = jax.tree.map(
        lambda part, kind: lax.all_gather(part.astype(kind), axis),
        array,
        jax.tree.map(lambda a: jnp.bfloat16 if a.dtype == jnp.float32 else a.dtype, array),
    )
    start = jax.tree.map(
        lambda part, zero: jnp.broadcast_to(jnp.asarray(zero, part.dtype), part.shape),
        array,
        identity,
    )

    def turn(k, before):
        at = count - 1 - k
        reached = at > place
        new = combine(
            before, jax.tree.map(lambda part, own: part[at].astype(own.dtype), everything, array)
        )
        return jax.tree.map(lambda a, b: jnp.where(reached, a, b), new, before)

    return lax.fori_loop(0, count, turn, start)


def wide_layer_norm(values, scale_vec, shift_vec):
    center = values - jnp.mean(values, axis=-1, keepdims=True)
    inverse = lax.rsqrt(jnp.mean(center * center, axis=-1, keepdims=True) + 1e-05)
    normed = center * inverse
    return (normed * scale_vec + shift_vec, normed, inverse)


def wide_norm_back(upstream, normed, inverse, scale_vec):
    scaled = upstream * scale_vec
    inner = (
        scaled
        - jnp.mean(scaled, axis=-1, keepdims=True)
        - normed * jnp.mean(scaled * normed, axis=-1, keepdims=True)
    )
    return (
        inverse * inner,
        jnp.sum(upstream * normed, axis=(0, 1)),
        jnp.sum(upstream, axis=(0, 1)),
    )


def shift_prev(values, persist_indicator):
    arrived = shifted(values[:, -1:, :], "tensor", 1)
    return jnp.concatenate([arrived, values[:, :-1]], axis=1) * persist_indicator[:, :, None]


def shift_back(upstream, persist_indicator):
    masked = upstream * persist_indicator[:, :, None]
    arrived = shifted(masked[:, :1, :], "tensor", -1)
    return jnp.concatenate([masked[:, 1:], arrived], axis=1)


def project(values, matrix):
    return jnp.einsum("rtd,de->rte", values, matrix, preferred_element_type=jnp.float32)


def project_back(upstream, matrix):
    return jnp.einsum("rte,de->rtd", upstream, matrix, preferred_element_type=jnp.float32)


def outer_sum(values, upstream):
    return jnp.einsum("rtd,rte->de", values, upstream, preferred_element_type=jnp.float32)


def mix_back(upstreams, shares, differ, persist_indicator):
    toward = jnp.zeros_like(differ)
    behind = jnp.zeros_like(differ)
    share_grads = []
    for upstream, share in zip(upstreams, shares):
        toward = toward + upstream * share
        behind = behind + upstream * (1.0 - share)
        share_grads.append(jnp.sum(upstream * differ, axis=(0, 1)))
    return (toward + shift_back(behind, persist_indicator), share_grads)


def chain_combine(earlier, later):
    return (
        earlier[0] * later[0],
        later[0] * earlier[1] + later[1],
        later[0] * earlier[2] + later[2],
    )


def scan_fragments(
    lookup_wide, payload_wide, fading_power, reward_coords, text_boundary_indicators
):
    decay_rate = jnp.exp(fading_power)
    row_count, span_len, width_len = lookup_wide.shape
    block_len = min(32, span_len)
    block_count = span_len // block_len
    places = jnp.arange(block_len, dtype=jnp.float32)
    rising = jnp.exp(places[:, None] * decay_rate)
    falling = jnp.exp(-(places[:, None] - 1.0) * decay_rate)
    trailing = jnp.exp(-(block_len - 1.0 - places)[:, None] * decay_rate)
    leading = jnp.exp(-places[:, None] * decay_rate)
    settle = jnp.exp(-block_len * decay_rate)
    before = places[:, None] > places[None, :]

    def split_blocks(values):
        return jnp.swapaxes(
            values.reshape((row_count, block_count, block_len) + values.shape[2:]), 0, 1
        )

    def advance(state_pair, scanned):
        accrued_dividend_sum, accrued_divisor_sum = state_pair
        lookup_narrow, payload_narrow, reset_b = scanned
        tree_levels = jnp.cumsum(reset_b, axis=1)
        linked = ((tree_levels[:, :, None] == tree_levels[:, None, :]) & before).astype(jnp.float32)
        key_term = jnp.exp(lookup_narrow)
        keyed_value = key_term * payload_narrow
        inside_numerator = falling * jnp.einsum(
            "rti,rid->rtd", linked, rising * keyed_value, precision=lax.Precision.HIGHEST
        )
        interior_divisor_sum = falling * jnp.einsum(
            "rti,rid->rtd", linked, rising * key_term, precision=lax.Precision.HIGHEST
        )
        leftover_multiplier = (tree_levels == 0).astype(jnp.float32)[:, :, None] * leading
        reward_multiplier = jnp.exp(reward_coords + lookup_narrow)
        above_total = (
            inside_numerator
            + reward_multiplier * payload_narrow
            + leftover_multiplier * accrued_dividend_sum[:, None, :]
        )
        below_total = (
            interior_divisor_sum
            + reward_multiplier
            + leftover_multiplier * accrued_divisor_sum[:, None, :]
        )
        ending = (tree_levels == tree_levels[:, -1:]).astype(jnp.float32)[:, :, None] * trailing
        intact = (tree_levels[:, -1] == 0).astype(jnp.float32)[:, None] * settle
        new_num = intact * accrued_dividend_sum + jnp.sum(ending * keyed_value, axis=1)
        new_den = intact * accrued_divisor_sum + jnp.sum(ending * key_term, axis=1)
        return ((new_num, new_den), (above_total, below_total))

    initial = jnp.zeros((row_count, width_len), jnp.float32)
    (total_num, total_den), (uppers, lowers) = lax.scan(
        advance,
        (initial, initial),
        (
            split_blocks(lookup_wide),
            split_blocks(payload_wide),
            split_blocks(text_boundary_indicators),
        ),
    )

    def join_blocks(values):
        return jnp.swapaxes(values, 0, 1).reshape(row_count, span_len, width_len)

    tree_levels = jnp.cumsum(text_boundary_indicators, axis=1)
    reaching = (tree_levels == 0).astype(jnp.float32)[:, :, None] * jnp.exp(
        -jnp.arange(span_len, dtype=jnp.float32)[:, None] * decay_rate
    )
    passing = (tree_levels[:, -1] == 0).astype(jnp.float32)[:, None] * jnp.exp(
        -span_len * decay_rate
    )
    return (join_blocks(uppers), join_blocks(lowers), reaching, total_num, total_den, passing)


def recurrence_finish(pieces_list, incoming_num, incoming_den):
    above_total = pieces_list[0] + pieces_list[2] * incoming_num[:, None, :]
    below_total = pieces_list[1] + pieces_list[2] * incoming_den[:, None, :]
    return (above_total / below_total, below_total)


def ffn_apply(inputs, key_weight, value_weight):
    hidden_pre = project(inputs, key_weight)
    hidden = jnp.square(jax.nn.relu(hidden_pre)).astype(jnp.bfloat16)
    return (hidden_pre, hidden, project(hidden, value_weight))


def ffn_grads(inputs, hidden_pre, hidden, upstream, key_weight, value_weight):
    g_hidden = jnp.einsum("rtd,fd->rtf", upstream, value_weight, preferred_element_type=jnp.float32)
    grad_value = jnp.einsum("rtf,rtd->fd", hidden, upstream, preferred_element_type=jnp.float32)
    g_pre = (2.0 * jax.nn.relu(hidden_pre) * g_hidden).astype(jnp.bfloat16)
    grad_key = jnp.einsum("rtd,rtf->df", inputs, g_pre, preferred_element_type=jnp.float32)
    g_inputs = jnp.einsum("rtf,df->rtd", g_pre, key_weight, preferred_element_type=jnp.float32)
    return (g_inputs, grad_key, grad_value)


def wide_shards(
    incoming_embeddings,
    text_boundary_indicators,
    upstream_sensitivity,
    primary_standardize_scaling,
    primary_standardize_offset,
    secondary_standardize_scaling,
    secondary_standardize_offset,
    feature_fading_logarithms,
    present_symbol_reward,
    timemix_lookup_blend,
    timemix_payload_blend,
    timemix_gate_blend,
    timemix_lookup_proj,
    timemix_payload_proj,
    timemix_gate_proj,
    timemix_emit_proj,
    feedmix_lookup_blend,
    feedmix_gate_blend,
    feedmix_gate_proj,
    feedmix_lookup_proj,
    feedmix_payload_proj,
):
    gathered_portions = (
        lax.all_gather(primary_standardize_scaling, ("dp", "tensor"), axis=0, tiled=True),
        lax.all_gather(primary_standardize_offset, ("dp", "tensor"), axis=0, tiled=True),
        lax.all_gather(secondary_standardize_scaling, ("dp", "tensor"), axis=0, tiled=True),
        lax.all_gather(secondary_standardize_offset, ("dp", "tensor"), axis=0, tiled=True),
        lax.all_gather(feature_fading_logarithms, ("dp", "tensor"), axis=0, tiled=True),
        lax.all_gather(present_symbol_reward, ("dp", "tensor"), axis=0, tiled=True),
        lax.all_gather(timemix_lookup_blend, ("dp", "tensor"), axis=0, tiled=True),
        lax.all_gather(timemix_payload_blend, ("dp", "tensor"), axis=0, tiled=True),
        lax.all_gather(timemix_gate_blend, ("dp", "tensor"), axis=0, tiled=True),
        lax.all_gather(timemix_lookup_proj, ("dp", "tensor"), axis=0, tiled=True),
        lax.all_gather(timemix_payload_proj, ("dp", "tensor"), axis=0, tiled=True),
        lax.all_gather(timemix_gate_proj, ("dp", "tensor"), axis=0, tiled=True),
        lax.all_gather(timemix_emit_proj, ("dp", "tensor"), axis=0, tiled=True),
        lax.all_gather(feedmix_lookup_blend, ("dp", "tensor"), axis=0, tiled=True),
        lax.all_gather(feedmix_gate_blend, ("dp", "tensor"), axis=0, tiled=True),
        lax.all_gather(feedmix_gate_proj, ("dp", "tensor"), axis=0, tiled=True),
    )
    initial_scaling_coords = gathered_portions[0].astype(jnp.float32)
    initial_offset_coords = gathered_portions[1].astype(jnp.float32)
    later_scaling_coords = gathered_portions[2].astype(jnp.float32)
    later_offset_coords = gathered_portions[3].astype(jnp.float32)
    fading_power = gathered_portions[4].astype(jnp.float32)
    reward_coords = gathered_portions[5].astype(jnp.float32)
    share_k1 = gathered_portions[6].astype(jnp.float32)
    share_v1 = gathered_portions[7].astype(jnp.float32)
    share_r1 = gathered_portions[8].astype(jnp.float32)
    lookup_coefficients_initial = gathered_portions[9]
    payload_coefficients_initial = gathered_portions[10]
    gate_coefficients_initial = gathered_portions[11]
    emit_coefficients_initial = gathered_portions[12]
    share_k2 = gathered_portions[13].astype(jnp.float32)
    share_r2 = gathered_portions[14].astype(jnp.float32)
    gate_coefficients_later = gathered_portions[15]
    lookup_coefficients_later, payload_coefficients_later = (
        lax.all_gather(feedmix_lookup_proj, "dp", axis=0, tiled=True),
        lax.all_gather(feedmix_payload_proj, "dp", axis=1, tiled=True),
    )
    persist_indicator = (1 - text_boundary_indicators).astype(jnp.float32)
    inputs = incoming_embeddings.astype(jnp.float32)
    normed_one, unit_one, inverse_one = wide_layer_norm(
        inputs, initial_scaling_coords, initial_offset_coords
    )
    prev_one = shift_prev(normed_one, persist_indicator)
    differ_one = normed_one - prev_one
    in_key = (prev_one + differ_one * share_k1).astype(jnp.bfloat16)
    in_value = (prev_one + differ_one * share_v1).astype(jnp.bfloat16)
    in_recept = (prev_one + differ_one * share_r1).astype(jnp.bfloat16)
    initial_lookup_lines = project(in_key, lookup_coefficients_initial)
    initial_payload_lines = project(in_value, payload_coefficients_initial)
    recept_one = project(in_recept, gate_coefficients_initial)
    pieces_list = scan_fragments(
        initial_lookup_lines,
        initial_payload_lines,
        fading_power,
        reward_coords,
        text_boundary_indicators,
    )
    passing = pieces_list[5]
    identity = (jnp.ones_like(passing), jnp.zeros_like(passing), jnp.zeros_like(passing))
    unused_item, incoming_num, incoming_den = carried_in(
        (passing, pieces_list[3], pieces_list[4]), "tensor", chain_combine, identity
    )
    blended_mean_state, below_total = recurrence_finish(pieces_list, incoming_num, incoming_den)
    sig_one = jax.nn.sigmoid(recept_one)
    mixed_att = (sig_one * blended_mean_state).astype(jnp.bfloat16)
    resid_one = inputs + project(mixed_att, emit_coefficients_initial)
    normed_two, unit_two, inverse_two = wide_layer_norm(
        resid_one, later_scaling_coords, later_offset_coords
    )
    prev_two = shift_prev(normed_two, persist_indicator)
    differ_two = normed_two - prev_two
    in_key_two = (prev_two + differ_two * share_k2).astype(jnp.bfloat16)
    in_recept_two = (prev_two + differ_two * share_r2).astype(jnp.bfloat16)
    recept_two = project(in_recept_two, gate_coefficients_later)
    sig_two = jax.nn.sigmoid(recept_two)
    row_inputs = lax.all_gather(in_key_two, "tensor", axis=1, tiled=True)
    hidden_pre, hidden, partial_value = ffn_apply(
        row_inputs, lookup_coefficients_later, payload_coefficients_later
    )
    value_two = lax.psum_scatter(
        partial_value.astype(jnp.bfloat16), "tensor", scatter_dimension=1, tiled=True
    ).astype(jnp.float32)
    layer_out = (resid_one + sig_two * value_two).astype(jnp.bfloat16)
    upstream = upstream_sensitivity.astype(jnp.float32)
    g_value_two = (upstream * sig_two).astype(jnp.bfloat16)
    g_recept_two = (upstream * value_two * sig_two * (1.0 - sig_two)).astype(jnp.bfloat16)
    grad_recept_two = outer_sum(in_recept_two, g_recept_two)
    g_mix_r2 = project_back(g_recept_two, gate_coefficients_later)
    row_grads = lax.all_gather(g_value_two, "tensor", axis=1, tiled=True)
    partial_grad, grad_key_two, grad_value_two = ffn_grads(
        row_inputs,
        hidden_pre,
        hidden,
        row_grads,
        lookup_coefficients_later,
        payload_coefficients_later,
    )
    g_mix_k2 = lax.psum_scatter(
        partial_grad.astype(jnp.bfloat16), "tensor", scatter_dimension=1, tiled=True
    ).astype(jnp.float32)
    sum_key_two, sum_value_two = (
        lax.psum_scatter(
            grad_key_two.astype(jnp.bfloat16), "dp", scatter_dimension=0, tiled=True
        ).astype(jnp.float32),
        lax.psum_scatter(
            grad_value_two.astype(jnp.bfloat16), "dp", scatter_dimension=1, tiled=True
        ).astype(jnp.float32),
    )
    g_normed_two, shares_two = mix_back(
        (g_mix_k2, g_mix_r2), (share_k2, share_r2), differ_two, persist_indicator
    )
    g_resid_part, grad_gain_two, grad_bias_two = wide_norm_back(
        g_normed_two, unit_two, inverse_two, later_scaling_coords
    )
    g_resid = upstream + g_resid_part
    g_branch = g_resid.astype(jnp.bfloat16)
    grad_out_one = outer_sum(mixed_att, g_branch)
    g_mixed = project_back(g_branch, emit_coefficients_initial)
    g_weighted = g_mixed * sig_one
    g_recept_one = (g_mixed * blended_mean_state * sig_one * (1.0 - sig_one)).astype(jnp.bfloat16)
    reaching = pieces_list[2]
    g_in_num = jnp.sum(g_weighted * reaching / below_total, axis=1)
    g_in_den = -jnp.sum(g_weighted * reaching * blended_mean_state / below_total, axis=1)
    unused_item, back_num, back_den = entering(
        (passing, g_in_num, g_in_den), "tensor", chain_combine, identity
    )
    g_passing = back_num * incoming_num + back_den * incoming_den

    def device_fragment(lookup_wide, payload_wide, fading_coords, reward_power):
        shard_pieces = scan_fragments(
            lookup_wide, payload_wide, fading_coords, reward_power, text_boundary_indicators
        )
        local_out, unused_item = recurrence_finish(shard_pieces, incoming_num, incoming_den)
        return (local_out, shard_pieces[3], shard_pieces[4], shard_pieces[5])

    unused_item, reverse_pass_rule = jax.vjp(
        device_fragment, initial_lookup_lines, initial_payload_lines, fading_power, reward_coords
    )
    derivative_lookup_wide, derivative_payload_wide, fading_derivative, reward_derivative = (
        reverse_pass_rule((g_weighted, back_num, back_den, g_passing))
    )
    g_key_one = derivative_lookup_wide.astype(jnp.bfloat16)
    g_value_one = derivative_payload_wide.astype(jnp.bfloat16)
    grad_key_one = outer_sum(in_key, g_key_one)
    grad_value_one = outer_sum(in_value, g_value_one)
    grad_recept_one = outer_sum(in_recept, g_recept_one)
    g_mix_k1 = project_back(g_key_one, lookup_coefficients_initial)
    g_mix_v1 = project_back(g_value_one, payload_coefficients_initial)
    g_mix_r1 = project_back(g_recept_one, gate_coefficients_initial)
    g_normed_one, shares_one = mix_back(
        (g_mix_k1, g_mix_v1, g_mix_r1),
        (share_k1, share_v1, share_r1),
        differ_one,
        persist_indicator,
    )
    g_input_part, grad_gain_one, grad_bias_one = wide_norm_back(
        g_normed_one, unit_one, inverse_one, initial_scaling_coords
    )
    grad_tokens = g_resid + g_input_part
    summed = (
        lax.psum_scatter(grad_gain_one, ("dp", "tensor"), scatter_dimension=0, tiled=True),
        lax.psum_scatter(grad_bias_one, ("dp", "tensor"), scatter_dimension=0, tiled=True),
        lax.psum_scatter(grad_gain_two, ("dp", "tensor"), scatter_dimension=0, tiled=True),
        lax.psum_scatter(grad_bias_two, ("dp", "tensor"), scatter_dimension=0, tiled=True),
        lax.psum_scatter(fading_derivative, ("dp", "tensor"), scatter_dimension=0, tiled=True),
        lax.psum_scatter(reward_derivative, ("dp", "tensor"), scatter_dimension=0, tiled=True),
        lax.psum_scatter(shares_one[0], ("dp", "tensor"), scatter_dimension=0, tiled=True),
        lax.psum_scatter(shares_one[1], ("dp", "tensor"), scatter_dimension=0, tiled=True),
        lax.psum_scatter(shares_one[2], ("dp", "tensor"), scatter_dimension=0, tiled=True),
        lax.psum_scatter(grad_key_one, ("dp", "tensor"), scatter_dimension=0, tiled=True),
        lax.psum_scatter(grad_value_one, ("dp", "tensor"), scatter_dimension=0, tiled=True),
        lax.psum_scatter(grad_recept_one, ("dp", "tensor"), scatter_dimension=0, tiled=True),
        lax.psum_scatter(grad_out_one, ("dp", "tensor"), scatter_dimension=0, tiled=True),
        lax.psum_scatter(shares_two[0], ("dp", "tensor"), scatter_dimension=0, tiled=True),
        lax.psum_scatter(shares_two[1], ("dp", "tensor"), scatter_dimension=0, tiled=True),
        lax.psum_scatter(grad_recept_two, ("dp", "tensor"), scatter_dimension=0, tiled=True),
    )
    return (
        layer_out,
        grad_tokens,
        summed[0],
        summed[1],
        summed[2],
        summed[3],
        summed[4],
        summed[5],
        summed[6],
        summed[7],
        summed[8],
        summed[9],
        summed[10],
        summed[11],
        summed[12],
        summed[13],
        summed[14],
        summed[15],
        sum_key_two,
        sum_value_two,
    )


def split_columns(w, parts):
    rows, width = w.shape
    return w.reshape(rows, parts, 2, width // (2 * parts)).transpose(2, 0, 1, 3).reshape(2, rows, width // 2)


def join_columns(own, other, c, parts):
    rows, half = own.shape[-2:]
    a = jnp.where(c == 0, own, other).reshape(own.shape[:-1] + (parts, half // parts))
    b = jnp.where(c == 0, other, own).reshape(own.shape[:-1] + (parts, half // parts))
    return jnp.stack([a, b], axis=-2).reshape(own.shape[:-1] + (2 * half,))


def pack(tokens, starts, upstream, gain1, bias1, gain2, bias2, fading, reward, mk1, mv1, mr1, wk, wv, wr, wo, mk2, mr2, wg, fk, fv):
    i, c, count = lax.axis_index("dp"), lax.axis_index("tensor"), lax.axis_size("dp")
    own_rows, width = wk.shape
    half, hidden = width // 2, fk.shape[1]
    by_core = jnp.stack([split_columns(wk, count), split_columns(wv, count), split_columns(wr, count), split_columns(wg, 1)])
    own4 = lax.dynamic_index_in_dim(by_core, c, 1, False)
    other4 = lax.dynamic_index_in_dim(by_core, 1 - c, 1, False)
    emit = wo.reshape(own_rows, 2, half).transpose(1, 0, 2).reshape(1, 2 * own_rows, half)
    key4 = fk.reshape(2 * own_rows, 4, hidden // 4).transpose(1, 0, 2)
    value4 = fv.reshape(4, hidden // 4, 2 * own_rows).transpose(0, 2, 1)
    chunks = {**{p: key4[j] for j, p in enumerate(KEYS)}, **{p: value4[j] for j, p in enumerate(VALUES)}}
    rest = jnp.concatenate([emit, jnp.stack([chunks[p] for p in range(FFN, PIECES)])])
    slots = 128 // own_rows
    everywhere = jnp.stack([gain1, bias1, gain2, bias2, fading, reward, mk1, mv1, mr1, mk2, mr2])
    own = jnp.stack([fading, reward, jnp.zeros_like(fading), jnp.zeros_like(fading), jnp.zeros_like(fading)])
    lane = jnp.arange(128)[None, :] // own_rows
    vec = jnp.concatenate([
        jnp.where(lane == (2 * i + c) % slots, jnp.tile(everywhere, (1, slots)), 0),
        jnp.where(lane == i % slots, jnp.tile(own, (1, slots)), 0),
    ]).astype(BF16)
    keep = jnp.broadcast_to((1 - starts[0]).astype(F32)[:, None], (starts.shape[1], 128))
    return own4, other4, rest, vec, tokens[0], upstream[0], keep


def shards(*args):
    tokens = args[0]
    c = lax.axis_index("tensor")
    i = lax.axis_index("dp")
    count = lax.axis_size("dp")
    own_rows, width = args[12].shape
    hidden = args[19].shape[1]
    half = width // 2
    (
        g, layer_out, x, up, ins, kvr, sn, sd, mixed, resid, ins2, pre, act, g_value, g_recept2, vec, rows, keep,
    ) = forward_call(*pack(*args))

    total, recv4, vsum, vother, grad_tokens = backward_call(
        g, x, up, ins, kvr, sn, sd, mixed, resid, ins2, pre, act, g_value, g_recept2, vec, rows, keep
    )
    slots = 128 // own_rows
    vtotal = lax.dynamic_slice_in_dim(vsum + vother, (2 * i + c) % slots * own_rows, own_rows, 1)
    own_scan = lax.dynamic_slice_in_dim(vsum, i % slots * own_rows, own_rows, 1)
    own = lax.dynamic_slice_in_dim(total[R_GATE2:], c * own_rows, own_rows, 1)
    out_k, out_v, out_r = (join_columns(own[2 + n], recv4[n], c, count) for n in range(3))
    out_g = join_columns(own[0], recv4[3], c, 1)
    out_o = total[R_EMIT].reshape(2, own_rows, half).transpose(1, 0, 2).reshape(own_rows, width)
    out_fk = total[R_KEY : R_KEY + 4].transpose(1, 0, 2).reshape(2 * own_rows, hidden)
    out_fv = total[R_VALUE : R_VALUE + 4].transpose(0, 2, 1).reshape(hidden, 2 * own_rows)
    return (
        layer_out[None], grad_tokens[None], *(vtotal[n] for n in range(4)), own_scan[SUMS], own_scan[SUMS + 1],
        *(vtotal[n] for n in range(6, 9)), out_k, out_v, out_r, out_o, vtotal[9], vtotal[10], out_g, out_fk, out_fv,
    )


def solution(mesh):
    row, vector, matrix_ = P("dp", "tensor", None), P(("dp", "tensor")), P(("dp", "tensor"), None)
    key, value = P("dp", "tensor"), P("tensor", "dp")
    in_specs = (row, P("dp", "tensor"), row) + (vector,) * 9 + (matrix_,) * 4 + (vector,) * 2 + (matrix_, key, value)
    out_specs = (row, row) + (vector,) * 9 + (matrix_,) * 4 + (vector,) * 2 + (matrix_, key, value)
    body = shards if (mesh.shape["dp"], mesh.shape["tensor"]) == (16, 2) else wide_shards
    return jax.shard_map(body, mesh=mesh, in_specs=in_specs, out_specs=out_specs, check_vma=False)
```

profile of v0, /device:TPU:0, one launch (start us, length us, event | category | flops | bytes accessed | tf_op | source)
XLA Modules:
  0.0 267.6 jit_solution(7021541335171019304)
XLA Ops:
  0.7 0.9 reshape.299
  1.6 1.1 reshape.298
  2.7 0.0 copy-start.4
  2.7 0.2 stack_reshape.10
  3.0 1.1 reshape.297
  4.0 0.0 copy-start.5
  4.1 0.2 stack_reshape.9
  4.3 0.2 reshape.296
  4.5 0.0 copy-start.9
  4.5 0.0 copy-start.10
  4.6 0.0 copy-start.12
  4.7 0.2 stack_reshape.8
  5.0 0.7 dynamic-slice_bitcast_fusion
  6.0 0.1 pad.13.clone
  6.0 0.1 pad.12.clone
  6.1 0.1 maximum_maximum_fusion
  6.2 0.1 tile.21
  6.4 0.1 stack.71
  6.5 0.1 tile.9
  6.6 0.6 pad_maximum_fusion.5.vec
  7.2 0.8 broadcast_in_dim.41.keep_own
  8.0 122.4 %forward.1 = (bf16[13,4,4,64,512]{4,3,2,1,0:T(8,128)(2,1)}, bf16[512,1024]{1,0:T(8,128)(2,1)}, bf16[1024,1024]{1,0:T(8,128)(2,1)}, bf16[1024,1024]{1,0:T(8,128)(...) custom-call(bf16[4,32,512]{2,1,0:T(8,128)(2,1)} %get-tuple-element.7, ...), custom_call_target="tpu_custom_call" | custom-call | tf_op jit(solution)/shard_map/forward/pallas_call | solution.py:814
  130.4 120.7 %backward.1 = (f32[13,64,512]{2,1,0:T(8,128)}, f32[4,32,512]{2,1,0:T(8,128)}, f32[16,128]{1,0:T(8,128)}, f32[16,128]{1,0:T(8,128)}, f32[512,1024]{1,0:T(8,128)}) custom-call(bf16[13,4,4,64,512]{4,3,2,1,0:T(8,128)(2,1)} %get-tuple-element.44.g, bf16[1024,1024]{1,0:T(8,128)(2,1)} %get-tuple-element.45.x_in, bf16[1024,1024]{1,0:T(8,128)(2,1)} %get-tuple-element.46.up_in, ...), custom_call_target="tpu_custom_call" | custom-call | tf_op jit(solution)/shard_map/backward/pallas_call | solution.py:1291
  251.1 0.8 dynamic-slice_add_fusion
  251.9 0.6 slice_bitcast_fusion.2
  252.5 1.3 dynamic-slice_bitcast_fusion.2
  253.8 1.1 slice.110
  255.0 1.0 select_bitcast_fusion.1
  256.0 0.1 select_n.184
  256.1 0.1 select_n.182
  256.3 0.4 copy.57
  256.7 1.3 reshape.304
  258.0 0.1 select_n.188
  258.1 0.1 select_n.186
  258.3 0.4 copy.58
  258.7 1.3 reshape.305
  260.0 0.1 select_n.192
  260.2 0.1 select_n.190
  260.3 0.4 copy.59
  260.7 1.3 reshape.306
  262.1 0.7 copy.67
  262.7 0.1 copy.61
  262.9 0.7 copy.70
  263.5 0.1 slice_bitcast_fusion
  263.7 0.8 copy.68
  264.5 0.8 copy.69
  265.3 1.0 copy.89
  266.3 1.3 copy.90
  (64 shorter events, 0.5 us)
Async XLA Ops:
  0.7 3.7 %copy-start.6 = (bf16[32,1024]{1,0:T(8,128)(2,1)S(1)}, bf16[32,1024]{1,0:T(8,128)(2,1)}, u32[]{:S(2)}) copy-start(bf16[32,1024]{1,0:T(8,128)(2,1)} %param.33) | copy-start | bytes 196612
  2.7 3.1 %copy-start.7 = (bf16[32,1024]{1,0:T(8,128)(2,1)S(1)}, bf16[32,1024]{1,0:T(8,128)(2,1)}, u32[]{:S(2)}) copy-start(bf16[32,1024]{1,0:T(8,128)(2,1)} %param.36) | copy-start | bytes 196612
  2.7 3.0 %copy-start.4 = (bf16[64,2048]{1,0:T(8,128)(2,1)S(1)}, bf16[64,2048]{1,0:T(8,128)(2,1)}, u32[]{:S(2)}) copy-start(bf16[64,2048]{1,0:T(8,128)(2,1)} %param.40) | copy-start | bytes 786436
  4.0 1.8 copy-start.5
  4.5 1.6 copy-start.9
  4.5 1.6 copy-start.10
  4.6 1.8 copy-start.11
  4.6 1.8 copy-start.12
  4.6 1.8 copy-start.13
  4.6 1.8 copy-start.14
  4.6 1.8 copy-start.15
  4.6 1.8 copy-start.16
  4.6 1.7 copy-start.17
  4.6 1.7 copy-start.18
  4.7 1.7 copy-start.19
  4.7 2.5 copy-start.8
  5.9 2.1 copy-start.3
  258.7 3.4 %copy-start.1 = (f32[13,64,512]{2,1,0:T(8,128)S(1)}, f32[13,64,512]{2,1,0:T(8,128)}, u32[]{:S(2)}) copy-start(f32[13,64,512]{2,1,0:T(8,128)} %get-tuple-element.64) | copy-start | bytes 5111812
  263.5 1.8 copy-start.2
  263.7 2.7 copy-start
where the time goes:
time: 268 us
  Pallas kernels  243 us (91%)
  local copies, waits for them, and re-layouts  20.6 us (8%)
    pallas_call x1, Pallas kernels, forward_call(): pl.pallas_call(forward_kernel, out_shape=tuple((o[0] for o in outs)), in_...  122 us
    pallas_call x1, Pallas kernels, backward_call(): pl.pallas_call(functools.partial(backward_kernel, PLAN), out_shape=(shape...  121 us

commit v1 on v0

--- a/solution.py
+++ b/solution.py
@@ -190,6 +190,14 @@
         own = self.part().at[a, yx]
         self.add_up(own, others, own)
 
+    def give(self, others):
+        start = 0
+        for out in self.out:
+            rows = pl.ds(start, out.shape[0])
+            own = self.part().at[self.z, self.yx, rows]
+            self.add_up(own, [other.at[rows] for other in others], out)
+            start += out.shape[0]
+
     def stage1(self):
         self.start(self.diagonal())
 
@@ -216,7 +224,7 @@
 
     def stage4(self):
         self.arrive(self.down())
-        self.add_up(self.part().at[self.z, self.yx], [self.line.at[k] for k in range(3)], self.out)
+        self.give([self.line.at[k] for k in range(3)])
 
     def finish(self):
         for copy in self.diagonal() + self.side() + self.down():
@@ -293,7 +301,7 @@
 
     def stage6(self):
         self.arrive(self.sides())
-        self.add_up(self.part().at[self.z, self.yx], [self.ring2.at[0], self.ring2.at[1]], self.out)
+        self.give([self.ring2.at[0], self.ring2.at[1]])
 
     def finish(self):
         for k in (1, 2, 3):
@@ -503,11 +511,35 @@
     lax.fori_loop(0, length // TILE, step, jnp.zeros((1, width), F32))
 
 
+def unweave(ref, own, other, c):
+    at = lax.broadcasted_iota(jnp.int32, (ref.shape[0], 128), 1) // 32
+    for t in range(own.shape[1] // 128):
+        a, b = ref[:, lanes(2 * t)].astype(F32), ref[:, lanes(2 * t + 1)].astype(F32)
+        a3, a2, b2, b1 = pltpu.roll(a, 96, 1), pltpu.roll(a, 64, 1), pltpu.roll(b, 64, 1), pltpu.roll(b, 32, 1)
+        first = jnp.where(at == 0, a, jnp.where(at == 1, a3, jnp.where(at == 2, b2, b1)))
+        second = jnp.where(at == 0, a3, jnp.where(at == 1, a2, jnp.where(at == 2, b1, b)))
+        own[:, lanes(t)] = jnp.where(c == 0, first, second).astype(BF16)
+        other[:, lanes(t)] = jnp.where(c == 0, second, first).astype(BF16)
+
+
+def weave(a, b, out):
+    at = lax.broadcasted_iota(jnp.int32, (out.shape[0], 128), 1) // 32
+    for t in range(out.shape[1] // 128):
+        p, q = a[:, lanes(t // 2)], b[:, lanes(t // 2)]
+        if t % 2 == 0:
+            turned = (p, pltpu.roll(q, 32, 1), pltpu.roll(p, 32, 1), pltpu.roll(q, 64, 1))
+        else:
+            turned = (pltpu.roll(p, 64, 1), pltpu.roll(q, 96, 1), pltpu.roll(p, 96, 1), q)
+        out[:, lanes(t)] = jnp.where(
+            at == 0, turned[0], jnp.where(at == 1, turned[1], jnp.where(at == 2, turned[2], turned[3]))
+        )
+
+
 def forward_kernel(
-    own4, other4, rest, vec, x_own, up_own, keep_own,
+    wk, wv, wr, wg, wo, fk, fvt, vec, x_own, up_own, keep_own,
     g_out, out, x_out, up_out, ins_out, kvr_out, sn_out, sd_out, mixed_out, resid_out, ins2_out, pre_out, act_out,
     gv_out, gr_out, vec_out, rows_out, keep_out,
-    gv, g, x, up, ins, kvr, sn, sd, mixed, sum_own, sum_other, resid, ins2, pre, act, v_send, v_other, gval, grec, low_half,
+    own3, other3, gv, g, x, up, ins, kvr, sn, sd, mixed, sum_own, sum_other, resid, ins2, pre, act, v_send, v_other, gval, grec, low_half,
     local_sem, ex_send, ex_recv, sends, recvs, lsends, lrecvs, vsends, vrecvs, out_sem, sum_send, sum_recv, val_send, val_recv,
 ):
     z, yx, c = place()
@@ -515,15 +547,17 @@
     half = width // 2
     span = length // 2
     partner = (z * 4 + yx, 1 - c)
+    for n, ref in enumerate((wk, wv, wr)):
+        unweave(ref, own3.at[n], other3.at[n], c)
     enter(z, yx, c)
 
-    block = own4.shape[1]
+    block = wk.shape[0]
     mine = strip(c, block)
     rows_mine = strip(c, span)
     swaps = [
         (vec, gv.at[z, yx, c]),
-        (other4.at[0:3], g.at[0:3, z, yx, mine]),
-        (other4.at[3], g.at[GATE2, z, yx, mine]),
+        (other3, g.at[0:3, z, yx, mine]),
+        (wg.at[:, strip(1 - c, half)], g.at[GATE2, z, yx, mine]),
         (x_own, x.at[rows_mine]),
         (keep_own, keep_out.at[rows_mine]),
         (up_own, up.at[rows_mine]),
@@ -531,14 +565,18 @@
     swaps = [remote(a, b, ex_send.at[n], ex_recv.at[n], partner) for n, (a, b) in enumerate(swaps)]
     keeps = [
         (vec, gv.at[z, yx, c]),
-        (own4.at[0:3], g.at[0:3, z, yx, mine]),
-        (own4.at[3], g.at[GATE2, z, yx, mine]),
+        (own3, g.at[0:3, z, yx, mine]),
+        (wg.at[:, strip(c, half)], g.at[GATE2, z, yx, mine]),
         (x_own, x.at[rows_mine]),
         (keep_own, keep_out.at[rows_mine]),
         (up_own, up.at[rows_mine]),
-        (rest.at[0], g.at[EMIT, z, yx]),
-        (rest.at[1:9], g.at[FFN : FFN + 8, z, yx]),
     ]
+    for h in range(2):
+        keeps.append((wo.at[:, h * half : (h + 1) * half], g.at[EMIT, z, yx, h * block : (h + 1) * block]))
+    for n in range(4):
+        chunk = slice(n * half, (n + 1) * half)
+        keeps.append((fk.at[:, chunk], g.at[KEYS[n], z, yx]))
+        keeps.append((fvt.at[:, chunk], g.at[VALUES[n], z, yx]))
     keeps = [pltpu.make_async_copy(a, b, local_sem.at[n]) for n, (a, b) in enumerate(keeps)]
     for copy in swaps + keeps:
         copy.start()
@@ -780,10 +818,10 @@
             copy.wait()
 
 
-def forward_call(own4, other4, rest, vec, x_own, up_own, keep_own):
+def forward_call(wk, wv, wr, wg, wo, fk, fvt, vec, x_own, up_own, keep_own):
     span, width = x_own.shape
     length, half = 2 * span, width // 2
-    block = rest.shape[1:]
+    block = (fk.shape[0], half)
     any_, vmem = pl.BlockSpec(memory_space=pl.ANY), pl.BlockSpec(memory_space=pltpu.VMEM)
     full, col = (length, width), (length, half)
 
@@ -814,9 +852,11 @@
     return pl.pallas_call(
         forward_kernel,
         out_shape=tuple(o[0] for o in outs),
-        in_specs=[vmem] * 7,
+        in_specs=[vmem] * 11,
         out_specs=tuple(o[1] for o in outs),
         scratch_shapes=[
+            pltpu.VMEM((3, block[0] // 2, half), BF16),
+            pltpu.VMEM((3, block[0] // 2, half), BF16),
             pltpu.VMEM((4, 4, 2) + vec.shape, BF16),
             pltpu.VMEM((PIECES, 4, 4) + block, BF16),
             pltpu.VMEM(full, BF16),
@@ -837,7 +877,7 @@
             pltpu.VMEM((2,) + col, BF16),
             pltpu.VMEM(col, BF16),
             pltpu.VMEM(col, BF16),
-            dma((8,)), dma((6,)), dma((6,)),
+            dma((16,)), dma((6,)), dma((6,)),
             dma((RINGS, 7)), dma((RINGS, 7)), dma((PIECES - RINGS, 10)), dma((PIECES - RINGS, 10)), dma((1, 7)), dma((1, 7)),
             dma((40,)), dma((4,)), dma((4,)), dma((9,)), dma((9,)),
         ],
@@ -845,7 +885,7 @@
             collective_id=0, has_side_effects=True, vmem_limit_bytes=63 * MIB
         ),
         name="forward",
-    )(own4, other4, rest, vec, x_own, up_own, keep_own)
+    )(wk, wv, wr, wg, wo, fk, fvt, vec, x_own, up_own, keep_own)
 
 
 R_VALUE, R_KEY, R_GATE2, R_EMIT, R_TIME = 0, 4, 8, 9, 10
@@ -885,7 +925,8 @@
     plan,
     g, x_in, up_in, ins_in, kvr_in, sn_in, sd_in, mixed_in, resid_in, ins2_in, pre_in, act_in, gv_in, gr_in,
     vec, rows, keep,
-    out, recv4, vsum, vother, gtok,
+    out_k, out_v, out_r, out_g, out_o, out_fk, out_fv, vsum, vother, gtok,
+    own_t, recv_t, own_g,
     part, ring1, ring2, line, lring1, lring2, lline, vpart, vring1, vring2, vline,
     b, w, f, resid, sum_other, n1_other, acc, own_sums,
     load_sem, w_sem, sends, recvs, lsends, lrecvs, vsends, vrecvs, ex_send, ex_recv, sum_send, sum_recv,
@@ -940,24 +981,31 @@
     load("resid", resid_in, resid)
     enter(z, yx, c)
 
+    columns = strip(c, half)
+    outs = {R_GATE2: [own_g], R_EMIT: [out_o.at[:, h * half : (h + 1) * half] for h in range(2)]}
+    for n in range(4):
+        chunk = slice(n * half, (n + 1) * half)
+        outs[R_VALUE + n], outs[R_KEY + n] = [out_fv.at[:, chunk]], [out_fk.at[:, chunk]]
+    for n in range(3):
+        outs[R_TIME + n] = [own_t.at[n]]
     sums = []
     for p in range(PIECES):
         if p in LINED:
             n = LINED.index(p)
             sums.append(
                 ReduceLine(
-                    part, p % PARTS, lring1.at[n], lring2.at[n], lline.at[n], out.at[p], lsends.at[n], lrecvs.at[n]
+                    part, p % PARTS, lring1.at[n], lring2.at[n], lline.at[n], outs[p], lsends.at[n], lrecvs.at[n]
                 )
             )
         else:
             n = p - sum(q < p for q in LINED)
             sums.append(
-                Reduce(part, p % PARTS, ring1.at[n], ring2.at[n], line.at[n], out.at[p], sends.at[n], recvs.at[n])
+                Reduce(part, p % PARTS, ring1.at[n], ring2.at[n], line.at[n], outs[p], sends.at[n], recvs.at[n])
             )
-    vector_sums = Reduce(vpart, 0, vring1, vring2, vline, vsum, vsends, vrecvs)
+    vector_sums = Reduce(vpart, 0, vring1, vring2, vline, [vsum], vsends, vrecvs)
     final = []
-    rows4 = recv4.shape[1]
-    others = strip(1 - c, rows4)
+    rows4 = recv_t.shape[1]
+    mine, others = strip(c, rows4), strip(1 - c, rows4)
 
     def pump(name):
         for stage, p in plan[name]:
@@ -967,8 +1015,11 @@
             getattr(sums[p], "stage%d" % stage)()
             if stage == 4 and p in (R_GATE2, R_TIME, R_TIME + 1, R_TIME + 2):
                 n = len(final)
-                slot = 3 if p == R_GATE2 else p - R_TIME
-                final.append(remote(out.at[p, others], recv4.at[slot], ex_send.at[n], ex_recv.at[n], partner))
+                if p == R_GATE2:
+                    src, dst = own_g.at[others], out_g.at[:, columns]
+                else:
+                    src, dst = own_t.at[p - R_TIME, others], recv_t.at[p - R_TIME]
+                final.append(remote(src, dst, ex_send.at[n], ex_recv.at[n], partner))
                 final[-1].start()
 
     def gradient(p, lhs, rhs):
@@ -1225,8 +1276,12 @@
     for p in range(PIECES - PARTS, PIECES):
         sums[p].finish()
     vector_sums.finish()
+    out_g[:, columns] = own_g[mine, :]
     for copy in final + [swap]:
         copy.wait()
+    for n, out in enumerate((out_k, out_v, out_r)):
+        own, other = own_t[n, mine, :], recv_t[n]
+        weave(jnp.where(c == 0, own, other), jnp.where(c == 0, other, own), out)
 
 
 PLAN = {
@@ -1291,12 +1346,15 @@
     return pl.pallas_call(
         functools.partial(backward_kernel, PLAN),
         out_shape=(
-            shape(PIECES, *block), shape(4, block[0] // 2, block[1]), shape(16, 128), shape(16, 128),
+            *[shape(block[0] // 2, 2 * half)] * 5, *[shape(block[0], 4 * half)] * 2, shape(16, 128), shape(16, 128),
             shape(length // 2, 2 * half),
         ),
         in_specs=[any_] * 14 + [vmem] * 3,
-        out_specs=(vmem,) * 5,
+        out_specs=(vmem,) * 10,
         scratch_shapes=[
+            pltpu.VMEM((3,) + block, F32),
+            pltpu.VMEM((3, block[0] // 2, block[1]), F32),
+            pltpu.VMEM(block, F32),
             pltpu.VMEM((PARTS, 4, 4) + block, BF16),
             pltpu.VMEM((rings, 2, 2) + block, BF16),
             pltpu.VMEM((rings, 2, 4) + block, BF16),
@@ -1760,30 +1818,9 @@
     )
 
 
-def split_columns(w, parts):
-    rows, width = w.shape
-    return w.reshape(rows, parts, 2, width // (2 * parts)).transpose(2, 0, 1, 3).reshape(2, rows, width // 2)
-
-
-def join_columns(own, other, c, parts):
-    rows, half = own.shape[-2:]
-    a = jnp.where(c == 0, own, other).reshape(own.shape[:-1] + (parts, half // parts))
-    b = jnp.where(c == 0, other, own).reshape(own.shape[:-1] + (parts, half // parts))
-    return jnp.stack([a, b], axis=-2).reshape(own.shape[:-1] + (2 * half,))
-
-
 def pack(tokens, starts, upstream, gain1, bias1, gain2, bias2, fading, reward, mk1, mv1, mr1, wk, wv, wr, wo, mk2, mr2, wg, fk, fv):
-    i, c, count = lax.axis_index("dp"), lax.axis_index("tensor"), lax.axis_size("dp")
-    own_rows, width = wk.shape
-    half, hidden = width // 2, fk.shape[1]
-    by_core = jnp.stack([split_columns(wk, count), split_columns(wv, count), split_columns(wr, count), split_columns(wg, 1)])
-    own4 = lax.dynamic_index_in_dim(by_core, c, 1, False)
-    other4 = lax.dynamic_index_in_dim(by_core, 1 - c, 1, False)
-    emit = wo.reshape(own_rows, 2, half).transpose(1, 0, 2).reshape(1, 2 * own_rows, half)
-    key4 = fk.reshape(2 * own_rows, 4, hidden // 4).transpose(1, 0, 2)
-    value4 = fv.reshape(4, hidden // 4, 2 * own_rows).transpose(0, 2, 1)
-    chunks = {**{p: key4[j] for j, p in enumerate(KEYS)}, **{p: value4[j] for j, p in enumerate(VALUES)}}
-    rest = jnp.concatenate([emit, jnp.stack([chunks[p] for p in range(FFN, PIECES)])])
+    i, c = lax.axis_index("dp"), lax.axis_index("tensor")
+    own_rows = wk.shape[0]
     slots = 128 // own_rows
     everywhere = jnp.stack([gain1, bias1, gain2, bias2, fading, reward, mk1, mv1, mr1, mk2, mr2])
     own = jnp.stack([fading, reward, jnp.zeros_like(fading), jnp.zeros_like(fading), jnp.zeros_like(fading)])
@@ -1793,36 +1830,26 @@
         jnp.where(lane == i % slots, jnp.tile(own, (1, slots)), 0),
     ]).astype(BF16)
     keep = jnp.broadcast_to((1 - starts[0]).astype(F32)[:, None], (starts.shape[1], 128))
-    return own4, other4, rest, vec, tokens[0], upstream[0], keep
+    return wk, wv, wr, wg, wo, fk, fv.T, vec, tokens[0], upstream[0], keep
 
 
 def shards(*args):
-    tokens = args[0]
     c = lax.axis_index("tensor")
     i = lax.axis_index("dp")
-    count = lax.axis_size("dp")
-    own_rows, width = args[12].shape
-    hidden = args[19].shape[1]
-    half = width // 2
+    own_rows = args[12].shape[0]
     (
         g, layer_out, x, up, ins, kvr, sn, sd, mixed, resid, ins2, pre, act, g_value, g_recept2, vec, rows, keep,
     ) = forward_call(*pack(*args))
 
-    total, recv4, vsum, vother, grad_tokens = backward_call(
+    out_k, out_v, out_r, out_g, out_o, out_fk, out_fv, vsum, vother, grad_tokens = backward_call(
         g, x, up, ins, kvr, sn, sd, mixed, resid, ins2, pre, act, g_value, g_recept2, vec, rows, keep
     )
     slots = 128 // own_rows
     vtotal = lax.dynamic_slice_in_dim(vsum + vother, (2 * i + c) % slots * own_rows, own_rows, 1)
     own_scan = lax.dynamic_slice_in_dim(vsum, i % slots * own_rows, own_rows, 1)
-    own = lax.dynamic_slice_in_dim(total[R_GATE2:], c * own_rows, own_rows, 1)
-    out_k, out_v, out_r = (join_columns(own[2 + n], recv4[n], c, count) for n in range(3))
-    out_g = join_columns(own[0], recv4[3], c, 1)
-    out_o = total[R_EMIT].reshape(2, own_rows, half).transpose(1, 0, 2).reshape(own_rows, width)
-    out_fk = total[R_KEY : R_KEY + 4].transpose(1, 0, 2).reshape(2 * own_rows, hidden)
-    out_fv = total[R_VALUE : R_VALUE + 4].transpose(0, 2, 1).reshape(hidden, 2 * own_rows)
     return (
         layer_out[None], grad_tokens[None], *(vtotal[n] for n in range(4)), own_scan[SUMS], own_scan[SUMS + 1],
-        *(vtotal[n] for n in range(6, 9)), out_k, out_v, out_r, out_o, vtotal[9], vtotal[10], out_g, out_fk, out_fv,
+        *(vtotal[n] for n in range(6, 9)), out_k, out_v, out_r, out_o, vtotal[9], vtotal[10], out_g, out_fk, out_fv.T,
     )
 
 

time: 268 us -> 262 us (0.978)
  local copies, waits for them, and re-layouts: 20.6 us -> 15 us
    reshape x14 -> x0, local copies, waits for them, and re-layouts: 9.58 us -> none  [the longest x3 3.97 us: join_columns(): return jnp.stack([a, b], axis=-2).reshape(own.shape[:-1] + (2 * half,))]
    unnamed x52 -> x23, local copies, waits for them, and re-layouts: 3.24 us -> 10.4 us
where the time goes in v1:
time: 262 us
  Pallas kernels  243 us (93%)
  local copies, waits for them, and re-layouts  15 us (6%)
  other arithmetic  2.95 us (1%)
    pallas_call x1, Pallas kernels, forward_call(): pl.pallas_call(forward_kernel, out_shape=tuple((o[0] for o in outs)), in_...  123 us
    pallas_call x1, Pallas kernels, backward_call(): pl.pallas_call(functools.partial(backward_kernel, PLAN), out_shape=(*[sha...  121 us
    unnamed x23, local copies, waits for them, and re-layouts  10.4 us

profile of v1, /device:TPU:0, one launch (start us, length us, event | category | flops | bytes accessed | tf_op | source)
XLA Modules:
  0.0 262.0 jit_solution(10613776891975226344)
XLA Ops:
  0.7 0.1 pad.5.clone
  0.7 0.1 pad.4.clone
  0.8 0.7 maximum_maximum_fusion
  1.6 0.1 tile.21
  1.7 1.5 stack.55
  3.2 0.1 tile.9
  3.3 0.6 pad_maximum_fusion.vec
  3.9 0.7 subtract_convert_fusion
  4.6 0.8 broadcast_in_dim.41.keep_own
  5.4 122.7 %forward.1 = (bf16[13,4,4,64,512]{4,3,2,1,0:T(8,128)(2,1)}, bf16[512,1024]{1,0:T(8,128)(2,1)}, bf16[1024,1024]{1,0:T(8,128)(2,1)}, bf16[1024,1024]{1,0:T(8,128)(...) custom-call(bf16[32,1024]{1,0:T(8,128)(2,1)} %wk.1, ...), custom_call_target="tpu_custom_call" | custom-call | tf_op jit(solution)/shard_map/forward/pallas_call | solution.py:852
  128.1 120.7 %backward.1 = (f32[32,1024]{1,0:T(8,128)}, f32[32,1024]{1,0:T(8,128)}, f32[32,1024]{1,0:T(8,128)}, f32[32,1024]{1,0:T(8,128)}, f32[32,1024]{1,0:T(8,128)}, /*ind...) custom-call(bf16[13,4,4,64,512]{4,3,2,1,0:T(8,128)(2,1)} %get-tuple-elem, ...), custom_call_target="tpu_custom_call" | custom-call | tf_op jit(solution)/shard_map/backward/pallas_call | solution.py:1346
  248.8 0.0 copy-start.6
  248.8 0.0 copy-start.5
  248.8 0.0 copy-start.4
  248.8 0.0 copy-start.3
  248.8 0.0 copy-start.2
  248.9 0.0 copy-start.1
  248.9 0.9 dynamic-slice_add_fusion
  249.8 0.6 slice_bitcast_fusion
  250.3 1.3 dynamic-slice_bitcast_fusion
  251.7 0.0 copy-start
  251.7 2.3 copy.50
  254.0 3.2 %copy.51 = f32[1,512,1024]{2,1,0:T(8,128)} copy(f32[1,512,1024]{2,1,0:T(8,128)} %bitcast.41) | data formatting | bytes 4194304
  257.1 0.0 copy-done.6
  257.1 0.7 copy.52
  257.8 0.0 copy-done.5
  257.8 0.7 copy.53
  258.5 0.0 copy-done.4
  258.5 0.7 copy.54
  259.1 0.0 copy-done.3
  259.1 0.7 copy.55
  259.8 0.0 copy-done.2
  259.8 0.7 copy.56
  260.4 0.0 copy-done.1
  260.4 0.8 copy.57
  261.2 0.0 copy-done
  261.2 0.8 copy.58
  (6 shorter events, 0.0 us)
Async XLA Ops:
  248.8 8.3 %copy-start.6 = (f32[32,1024]{1,0:T(8,128)S(1)}, f32[32,1024]{1,0:T(8,128)}, u32[]{:S(2)}) copy-start(f32[32,1024]{1,0:T(8,128)} %get-tuple-element.120) | copy-start | bytes 393220
  248.8 9.0 %copy-start.5 = (f32[32,1024]{1,0:T(8,128)S(1)}, f32[32,1024]{1,0:T(8,128)}, u32[]{:S(2)}) copy-start(f32[32,1024]{1,0:T(8,128)} %get-tuple-element.121) | copy-start | bytes 393220
  248.8 9.6 %copy-start.4 = (f32[32,1024]{1,0:T(8,128)S(1)}, f32[32,1024]{1,0:T(8,128)}, u32[]{:S(2)}) copy-start(f32[32,1024]{1,0:T(8,128)} %get-tuple-element.122) | copy-start | bytes 393220
  248.8 10.3 %copy-start.3 = (f32[32,1024]{1,0:T(8,128)S(1)}, f32[32,1024]{1,0:T(8,128)}, u32[]{:S(2)}) copy-start(f32[32,1024]{1,0:T(8,128)} %get-tuple-element.123) | copy-start | bytes 393220
  248.8 10.9 %copy-start.2 = (f32[32,1024]{1,0:T(8,128)S(1)}, f32[32,1024]{1,0:T(8,128)}, u32[]{:S(2)}) copy-start(f32[32,1024]{1,0:T(8,128)} %get-tuple-element.126) | copy-start | bytes 393220
  248.9 11.6 %copy-start.1 = (f32[64,2048]{1,0:T(8,128)S(1)}, f32[64,2048]{1,0:T(8,128)}, u32[]{:S(2)}) copy-start(f32[64,2048]{1,0:T(8,128)} %get-tuple-element.127) | copy-start | bytes 1572868
  251.7 9.6 %copy-start = (f32[64,2048]{1,0:T(8,128)S(1)}, f32[64,2048]{1,0:T(8,128)}, u32[]{:S(2)}) copy-start(f32[64,2048]{1,0:T(8,128)} %get-tuple-element.75) | copy-start | bytes 1572868

commit v2 on v1

--- a/solution.py
+++ b/solution.py
@@ -536,10 +536,10 @@
 
 
 def forward_kernel(
-    wk, wv, wr, wg, wo, fk, fvt, vec, x_own, up_own, keep_own,
+    wk, wv, wr, wg, wo, fk, fvt, vec, x_own, up_own, starts,
     g_out, out, x_out, up_out, ins_out, kvr_out, sn_out, sd_out, mixed_out, resid_out, ins2_out, pre_out, act_out,
     gv_out, gr_out, vec_out, rows_out, keep_out,
-    own3, other3, gv, g, x, up, ins, kvr, sn, sd, mixed, sum_own, sum_other, resid, ins2, pre, act, v_send, v_other, gval, grec, low_half,
+    own3, other3, keep_own, gv, g, x, up, ins, kvr, sn, sd, mixed, sum_own, sum_other, resid, ins2, pre, act, v_send, v_other, gval, grec, low_half,
     local_sem, ex_send, ex_recv, sends, recvs, lsends, lrecvs, vsends, vrecvs, out_sem, sum_send, sum_recv, val_send, val_recv,
 ):
     z, yx, c = place()
@@ -547,6 +547,7 @@
     half = width // 2
     span = length // 2
     partner = (z * 4 + yx, 1 - c)
+    keep_own[...] = jnp.broadcast_to(1.0 - starts[...].astype(F32), (128, span)).T
     for n, ref in enumerate((wk, wv, wr)):
         unweave(ref, own3.at[n], other3.at[n], c)
     enter(z, yx, c)
@@ -818,7 +819,7 @@
             copy.wait()
 
 
-def forward_call(wk, wv, wr, wg, wo, fk, fvt, vec, x_own, up_own, keep_own):
+def forward_call(wk, wv, wr, wg, wo, fk, fvt, vec, x_own, up_own, starts):
     span, width = x_own.shape
     length, half = 2 * span, width // 2
     block = (fk.shape[0], half)
@@ -857,6 +858,7 @@
         scratch_shapes=[
             pltpu.VMEM((3, block[0] // 2, half), BF16),
             pltpu.VMEM((3, block[0] // 2, half), BF16),
+            pltpu.VMEM((span, 128), F32),
             pltpu.VMEM((4, 4, 2) + vec.shape, BF16),
             pltpu.VMEM((PIECES, 4, 4) + block, BF16),
             pltpu.VMEM(full, BF16),
@@ -885,7 +887,7 @@
             collective_id=0, has_side_effects=True, vmem_limit_bytes=63 * MIB
         ),
         name="forward",
-    )(wk, wv, wr, wg, wo, fk, fvt, vec, x_own, up_own, keep_own)
+    )(wk, wv, wr, wg, wo, fk, fvt, vec, x_own, up_own, starts)
 
 
 R_VALUE, R_KEY, R_GATE2, R_EMIT, R_TIME = 0, 4, 8, 9, 10
@@ -1829,8 +1831,37 @@
         jnp.where(lane == (2 * i + c) % slots, jnp.tile(everywhere, (1, slots)), 0),
         jnp.where(lane == i % slots, jnp.tile(own, (1, slots)), 0),
     ]).astype(BF16)
-    keep = jnp.broadcast_to((1 - starts[0]).astype(F32)[:, None], (starts.shape[1], 128))
-    return wk, wv, wr, wg, wo, fk, fv.T, vec, tokens[0], upstream[0], keep
+    return wk, wv, wr, wg, wo, fk, fv.T, vec, tokens[0], upstream[0], starts
+
+
+def land_kernel(*refs):
+    count = (len(refs) - 2) // 3
+    ins, outs, held = refs[:count], refs[count : 2 * count], refs[2 * count : 3 * count]
+    came, left = refs[-2:]
+    first = [pltpu.make_async_copy(ins[n], held[n], came.at[n]) for n in range(count)]
+    second = [pltpu.make_async_copy(held[n], outs[n], left.at[n]) for n in range(count)]
+    for copy in first:
+        copy.start()
+    for one, other in zip(first, second):
+        one.wait()
+        other.start()
+    for copy in second:
+        copy.wait()
+
+
+def land(*arrays):
+    any_, count = pl.BlockSpec(memory_space=pl.ANY), len(arrays)
+    size = sum(a.size * a.dtype.itemsize for a in arrays)
+    return pl.pallas_call(
+        land_kernel,
+        out_shape=tuple(jax.ShapeDtypeStruct(a.shape, a.dtype) for a in arrays),
+        in_specs=[any_] * count,
+        out_specs=(any_,) * count,
+        scratch_shapes=[pltpu.VMEM(a.shape, a.dtype) for a in arrays] + [pltpu.SemaphoreType.DMA((count,))] * 2,
+        compiler_params=pltpu.CompilerParams(vmem_limit_bytes=63 * MIB),
+        cost_estimate=pl.CostEstimate(flops=0, transcendentals=0, bytes_accessed=2 * size),
+        name="land",
+    )(*arrays)
 
 
 def shards(*args):
@@ -1844,12 +1875,16 @@
     out_k, out_v, out_r, out_g, out_o, out_fk, out_fv, vsum, vother, grad_tokens = backward_call(
         g, x, up, ins, kvr, sn, sd, mixed, resid, ins2, pre, act, g_value, g_recept2, vec, rows, keep
     )
+    out_fv = out_fv.T
+    layer_out, grad_tokens, out_k, out_v, out_r, out_g, out_o, out_fk = land(
+        layer_out, grad_tokens, out_k, out_v, out_r, out_g, out_o, out_fk
+    )
     slots = 128 // own_rows
     vtotal = lax.dynamic_slice_in_dim(vsum + vother, (2 * i + c) % slots * own_rows, own_rows, 1)
     own_scan = lax.dynamic_slice_in_dim(vsum, i % slots * own_rows, own_rows, 1)
     return (
         layer_out[None], grad_tokens[None], *(vtotal[n] for n in range(4)), own_scan[SUMS], own_scan[SUMS + 1],
-        *(vtotal[n] for n in range(6, 9)), out_k, out_v, out_r, out_o, vtotal[9], vtotal[10], out_g, out_fk, out_fv.T,
+        *(vtotal[n] for n in range(6, 9)), out_k, out_v, out_r, out_o, vtotal[9], vtotal[10], out_g, out_fk, out_fv,
     )
 
 

time: 262 us -> 253 us (0.966)
  local copies, waits for them, and re-layouts: 15 us -> 3.8 us
  Pallas kernels: 243 us -> 247 us
    unnamed x23 -> x7, local copies, waits for them, and re-layouts: 10.4 us -> 0.81 us
    pallas_call x0 -> x1, Pallas kernels: none -> 3.81 us  [land(): pl.pallas_call(land_kernel, out_shape=tuple((jax.ShapeDtypeStruct(a.shape...]
where the time goes in v2:
time: 253 us
  Pallas kernels  247 us (98%)
  local copies, waits for them, and re-layouts  3.8 us (2%)
    pallas_call x1, Pallas kernels, forward_call(): pl.pallas_call(forward_kernel, out_shape=tuple((o[0] for o in outs)), in_...  123 us
    pallas_call x1, Pallas kernels, backward_call(): pl.pallas_call(functools.partial(backward_kernel, PLAN), out_shape=(*[sha...  121 us

profile of v2, /device:TPU:0, one launch (start us, length us, event | category | flops | bytes accessed | tf_op | source)
XLA Modules:
  0.0 253.2 jit_solution(16990946775770330935)
XLA Ops:
  0.7 0.1 pad.5.clone
  0.7 0.1 pad.4.clone
  0.8 0.7 maximum_maximum_fusion
  1.6 0.1 tile.21
  1.7 1.5 stack.55
  3.2 0.1 tile.9
  3.3 0.6 pad_maximum_fusion.vec
  3.9 122.7 %forward.1 = (bf16[13,4,4,64,512]{4,3,2,1,0:T(8,128)(2,1)}, bf16[512,1024]{1,0:T(8,128)(2,1)}, bf16[1024,1024]{1,0:T(8,128)(2,1)}, bf16[1024,1024]{1,0:T(8,128)(...) custom-call(bf16[32,1024]{1,0:T(8,128)(2,1)} %wk.1, ...), custom_call_target="tpu_custom_call" | custom-call | tf_op jit(solution)/shard_map/forward/pallas_call | solution.py:853
  126.6 120.7 %backward.1 = (f32[32,1024]{1,0:T(8,128)}, f32[32,1024]{1,0:T(8,128)}, f32[32,1024]{1,0:T(8,128)}, f32[32,1024]{1,0:T(8,128)}, f32[32,1024]{1,0:T(8,128)}, /*ind...) custom-call(bf16[13,4,4,64,512]{4,3,2,1,0:T(8,128)(2,1)} %get-tuple-elem, ...), custom_call_target="tpu_custom_call" | custom-call | tf_op jit(solution)/shard_map/backward/pallas_call | solution.py:1348
  247.3 0.0 copy-start.1
  247.4 0.0 copy-start.2
  247.4 0.0 copy-start
  247.4 3.8 %land.1 = (bf16[512,1024]{1,0:T(8,128)(2,1)}, f32[512,1024]{1,0:T(8,128)}, f32[32,1024]{1,0:T(8,128)}, f32[32,1024]{1,0:T(8,128)}, f32[32,1024]{1,0:T(8,128)}, /...) custom-call(bf16[512,1024]{1,0:T(8,128)(2,1)} %get-tuple-element.56.refs_0_, ...), custom_call_target="tpu_custom_call" | custom-call | bytes 8650752 | tf_op jit(solution)/shard_map/land/pallas_call | solution.py:1855
  251.2 0.0 copy-done.1
  251.2 0.0 copy-done.2
  251.2 0.1 dynamic-slice_add_fusion
  251.3 0.6 slice_bitcast_fusion
  251.8 0.6 dynamic-slice_bitcast_fusion
  252.4 0.0 copy-done
  252.4 0.8 copy.42
  (6 shorter events, 0.0 us)
Async XLA Ops:
  247.3 3.9 %copy-start.1 = (f32[16,128]{1,0:T(8,128)S(1)}, f32[16,128]{1,0:T(8,128)}, u32[]{:S(2)}) copy-start(f32[16,128]{1,0:T(8,128)} %get-tuple-element.83) | copy-start | bytes 24580
  247.4 3.9 %copy-start.2 = (f32[16,128]{1,0:T(8,128)S(1)}, f32[16,128]{1,0:T(8,128)}, u32[]{:S(2)}) copy-start(f32[16,128]{1,0:T(8,128)} %get-tuple-element.84) | copy-start | bytes 24580
  247.4 5.1 %copy-start = (f32[64,2048]{1,0:T(8,128)S(1)}, f32[64,2048]{1,0:T(8,128)}, u32[]{:S(2)}) copy-start(f32[64,2048]{1,0:T(8,128)} %get-tuple-element.91) | copy-start | bytes 1572868

commit v3 on v2

--- a/solution.py
+++ b/solution.py
@@ -176,15 +176,17 @@
             copy.wait_recv()
 
     def add_up(self, own, others, result):
+        size = min(64, own.shape[0])
+
         def step(i, carry):
-            at = strip(i, 16)
+            at = strip(i, size)
             total = own[at, :].astype(F32)
             for other in others:
                 total = total + other[at, :].astype(F32)
             result[at, :] = total.astype(result.dtype)
             return carry
 
-        lax.fori_loop(0, own.shape[0] // 16, step, 0)
+        lax.fori_loop(0, own.shape[0] // size, step, 0)
 
     def add(self, a, yx, others):
         own = self.part().at[a, yx]
@@ -593,7 +595,7 @@
         outs.append(copy)
         return copy
 
-    along_z = {4: [(0, 1)], 5: [(1, 1)], 6: [(0, 2)], 7: [(1, 2)], 8: [(0, 3)], 9: [(1, 3)]}
+    along_z = {3: [(0, 1)], 4: [(1, 1)], 5: [(0, 2)], 6: [(1, 2)], 7: [(0, 3)], 8: [(1, 3)]}
 
     def turn(n):
         if n < RINGS:
@@ -1030,7 +1032,7 @@
             part[p % PARTS, a] = rows_a.astype(BF16).reshape(part.shape[2:])
             return carry
 
-        lax.fori_loop(0, 4, block, 0)
+        lax.fori_loop(0, 4, block, 0, unroll=True)
 
     def thirds(ref, h):
         return ref[2 * h : 2 * h + 2].reshape(half, half)

time: 253 us -> 251 us (level)
    pallas_call x1, Pallas kernels: 121 us -> 118 us  [backward_call(): pl.pallas_call(functools.partial(backward_kernel, PLAN), out_shape=(*[sha...]
where the time goes in v3:
time: 251 us
  Pallas kernels  245 us (98%)
  local copies, waits for them, and re-layouts  3.8 us (2%)
    pallas_call x1, Pallas kernels, forward_call(): pl.pallas_call(forward_kernel, out_shape=tuple((o[0] for o in outs)), in_...  124 us
    pallas_call x1, Pallas kernels, backward_call(): pl.pallas_call(functools.partial(backward_kernel, PLAN), out_shape=(*[sha...  118 us

profile of v3, /device:TPU:0, one launch (start us, length us, event | category | flops | bytes accessed | tf_op | source)
XLA Modules:
  0.0 250.9 jit_solution(16685780742978900527)
XLA Ops:
  0.7 0.1 pad.5.clone
  0.7 0.1 pad.4.clone
  0.8 0.7 maximum_maximum_fusion
  1.6 0.1 tile.21
  1.7 1.5 stack.55
  3.2 0.1 tile.9
  3.3 0.6 pad_maximum_fusion.vec
  3.9 123.6 %forward.1 = (bf16[13,4,4,64,512]{4,3,2,1,0:T(8,128)(2,1)}, bf16[512,1024]{1,0:T(8,128)(2,1)}, bf16[1024,1024]{1,0:T(8,128)(2,1)}, bf16[1024,1024]{1,0:T(8,128)(...) custom-call(bf16[32,1024]{1,0:T(8,128)(2,1)} %wk.1, ...), custom_call_target="tpu_custom_call" | custom-call | tf_op jit(solution)/shard_map/forward/pallas_call | solution.py:855
  127.5 117.5 %backward.1 = (f32[32,1024]{1,0:T(8,128)}, f32[32,1024]{1,0:T(8,128)}, f32[32,1024]{1,0:T(8,128)}, f32[32,1024]{1,0:T(8,128)}, f32[32,1024]{1,0:T(8,128)}, /*ind...) custom-call(bf16[13,4,4,64,512]{4,3,2,1,0:T(8,128)(2,1)} %get-tuple-elem, ...), custom_call_target="tpu_custom_call" | custom-call | tf_op jit(solution)/shard_map/backward/pallas_call | solution.py:1350
  245.0 0.0 copy-start.1
  245.0 0.0 copy-start.2
  245.0 0.0 copy-start
  245.0 3.8 %land.1 = (bf16[512,1024]{1,0:T(8,128)(2,1)}, f32[512,1024]{1,0:T(8,128)}, f32[32,1024]{1,0:T(8,128)}, f32[32,1024]{1,0:T(8,128)}, f32[32,1024]{1,0:T(8,128)}, /...) custom-call(bf16[512,1024]{1,0:T(8,128)(2,1)} %get-tuple-element.56.refs_0_, ...), custom_call_target="tpu_custom_call" | custom-call | bytes 8650752 | tf_op jit(solution)/shard_map/land/pallas_call | solution.py:1857
  248.8 0.0 copy-done.1
  248.9 0.0 copy-done.2
  248.9 0.1 dynamic-slice_add_fusion
  248.9 0.6 slice_bitcast_fusion
  249.5 0.6 dynamic-slice_bitcast_fusion
  250.1 0.0 copy-done
  250.1 0.8 copy.42
  (6 shorter events, 0.0 us)
Async XLA Ops:
  245.0 3.9 %copy-start.1 = (f32[16,128]{1,0:T(8,128)S(1)}, f32[16,128]{1,0:T(8,128)}, u32[]{:S(2)}) copy-start(f32[16,128]{1,0:T(8,128)} %get-tuple-element.83) | copy-start | bytes 24580
  245.0 3.9 %copy-start.2 = (f32[16,128]{1,0:T(8,128)S(1)}, f32[16,128]{1,0:T(8,128)}, u32[]{:S(2)}) copy-start(f32[16,128]{1,0:T(8,128)} %get-tuple-element.84) | copy-start | bytes 24580
  245.0 5.1 %copy-start = (f32[64,2048]{1,0:T(8,128)S(1)}, f32[64,2048]{1,0:T(8,128)}, u32[]{:S(2)}) copy-start(f32[64,2048]{1,0:T(8,128)} %get-tuple-element.91) | copy-start | bytes 1572868
